TPU v7x, 32 devices: a whole 2x2x4 slice. The times are simulated.
32 devices in a mesh: group: 8 (over z, y), expert: 4 (over x, core).
Axes of the slice: x: 2, y: 2, z: 4, core: 2. Of those that a mesh axis runs over, the one named last changes fastest.
Arguments:
- train_inputs: float32 [32, 16, 1024], P(('group', 'expert')), as said below
- inv_factor: float32 [32, 1024, 1024], P(('group', 'expert')), as said below
- weights: float32 [32, 1024, 512], P(('group', 'expert')), as said below
- candidates: float32 [16, 4096], replicated, as said below
- test_ids: int32 [1024], replicated, may hold values from 0 to 4095
- basis: bfloat16 [512, 32768], P(None, ('group', 'expert')), may hold values from -0.25 to 0.25
- climatology: float32 [32768], P(('group', 'expert')), may hold values from -3 to 3
Outputs:
- field: bfloat16 [1024, 32768], P(None, ('group', 'expert'))
Inputs may be any that keep to these rules, and one draw needn't show every extreme that they name: inv_factor[e] is lower triangular with L L^T = K + 0.1 I inverted, where K[r, s] = exp(-0.5 |x_r - x_s|^2) over the columns of train_inputs[e]. `train_inputs`: entries of magnitude below 2. `candidates`: entries of magnitude below 2. `weights`: entries of magnitude at most 0.6 * sqrt(32).
All inputs are finite; a program needn't handle non-finite values.
Results may differ from a plain program's by a relative error of at most 0.0045.
Values may be sent and summed in bfloat16 or wider, within the bound.
No kernel may reach another device: no remote copies, remote signals or barrier semaphores. Data moves between devices by JAX's collectives and lax.ppermute only.
A program may use at most 64 MiB of HBM per device.

v0:
```python
import jax
import jax.numpy as jnp
from jax import lax
from jax.experimental import pallas as pl
from jax.experimental.pallas import tpu as pltpu
from jax.sharding import PartitionSpec as P


signal_var = 1.0
noise_var = 0.1
prior_var = signal_var + noise_var

AXES = ("group", "expert")
LANES = 128
EXTRA = 8
F32 = jnp.float32
BF16 = jnp.bfloat16


def split3(v):
    a = v.astype(BF16).astype(F32)
    b = (v - a).astype(BF16).astype(F32)
    c = ((v - a) - b).astype(BF16).astype(F32)
    return a, b, c


def row_iota(shape):
    return lax.broadcasted_iota(jnp.int32, shape, 0)


def pick_rows(rows, count, width):
    at = row_iota((count, width))
    out = jnp.zeros((count, width), F32)
    for i, row in enumerate(rows):
        out = jnp.where(at == i, row, out)
    return out


def column_to_row(col):
    return jnp.transpose(jnp.broadcast_to(col, (LANES, LANES)))[0:1, :]


def row_to_column(row):
    return jnp.transpose(jnp.broadcast_to(row, (LANES, LANES)))


def place():
    expert = lax.axis_index("expert")
    group = lax.axis_index("group")
    return (expert >> 1) & 1, expert & 1, group & 1


def make_experts_kernel(near_half):
    def kernel(ids, cand, train, inv, wts, send, keep, ids_s, cand_s, train_s, inv_s, w_s, x_s, k1_s, k2_s, sem):
        runs = train.shape[2]
        dims = train.shape[1]
        out = wts.shape[2]
        rows = k1_s.shape[0]
        blocks = rows // LANES
        tri = 256
        nt = runs // tri
        small = [
            pltpu.make_async_copy(train.at[0], train_s, sem.at[0]),
            pltpu.make_async_copy(ids, ids_s, sem.at[1]),
            pltpu.make_async_copy(cand, cand_s, sem.at[2]),
        ]
        big = [pltpu.make_async_copy(wts.at[0], w_s, sem.at[3])]
        for j in reversed(range(nt)):
            region = (pl.ds(j * tri, tri), pl.ds(0, (j + 1) * tri))
            big.append(pltpu.make_async_copy(inv.at[(0,) + region], inv_s.at[region], sem.at[4 + j]))
        for copy in small + big:
            copy.start()
        at_x, at_core, _ = place()
        at_half = at_x if near_half else 1 - at_x

        small[0].wait()
        x = train_s[...]
        x1, x2, x3 = split3(x)
        s1, s2, s3 = split3(-0.5 * jnp.sum(x * x, axis=0, keepdims=True))
        one = jnp.ones((1, runs), F32)
        tail = pick_rows((s1, s2, s3, one, one, one), 8, runs)
        pad = jnp.zeros((LANES - 6 * dims - 8, runs), F32)
        x_s[...] = jnp.concatenate((x1, x2, x1, x2, x3, x1, tail, pad), axis=0).astype(BF16)

        small[1].wait()
        small[2].wait()
        groups = cand.shape[1] // LANES
        quarter = blocks // 2
        for b in range(blocks):
            at_quarter = at_core if b >= quarter else 1 - at_core
            ident = ids_s[at_half * blocks + at_quarter * quarter + b % quarter]
            low = jnp.broadcast_to(ident & (LANES - 1), (dims, LANES))
            high = jnp.broadcast_to(ident // LANES, (dims, LANES))
            q = jnp.zeros((dims, LANES), F32)
            for g in range(groups):
                part = jnp.take_along_axis(
                    cand_s[:, g * LANES : (g + 1) * LANES], low, axis=1, mode="promise_in_bounds"
                )
                q = jnp.where(high == g, part, q)
            q1, q2, q3 = split3(q)
            t1, t2, t3 = split3(-0.5 * jnp.sum(q * q, axis=0, keepdims=True))
            unit = jnp.ones((1, LANES), F32)
            side = pick_rows((unit, unit, unit, t1, t2, t3), 8, LANES)
            rest = jnp.zeros((LANES - 6 * dims - 8, LANES), F32)
            stacked = jnp.concatenate((q1, q1, q2, q2, q1, q3, side, rest), axis=0)
            lhs = jnp.transpose(stacked).astype(BF16)
            expo = jnp.dot(lhs, x_s[...], preferred_element_type=F32)
            kern = signal_var * jnp.exp(expo)
            k1 = kern.astype(BF16)
            at = pl.ds(b * LANES, LANES)
            k1_s[at, :] = k1
            k2_s[at, :] = (kern - k1.astype(F32)).astype(BF16)

        for copy in big:
            copy.wait()
        total = jnp.zeros((rows, LANES), F32)
        means = []
        nt_dims = (((1,), (1,)), ((), ()))
        for j in reversed(range(nt)):
            depth = (j + 1) * tri
            a = inv_s[j * tri : depth, :depth]
            a1 = a.astype(BF16)
            a2 = (a - a1.astype(F32)).astype(BF16)
            white = (
                lax.dot_general(k1_s[:, :depth], a1, nt_dims, preferred_element_type=F32)
                + lax.dot_general(k2_s[:, :depth], a1, nt_dims, preferred_element_type=F32)
                + lax.dot_general(k1_s[:, :depth], a2, nt_dims, preferred_element_type=F32)
            )
            square = white * white
            for i in range(tri // LANES):
                total = total + square[:, i * LANES : (i + 1) * LANES]
            if len(means) * tri < out:
                w = w_s[:, len(means) * tri : (len(means) + 1) * tri]
                w1 = w.astype(BF16)
                w2 = (w - w1.astype(F32)).astype(BF16)
                means.append(
                    jnp.dot(k1_s[...], w1, preferred_element_type=F32)
                    + jnp.dot(k2_s[...], w1, preferred_element_type=F32)
                    + jnp.dot(k1_s[...], w2, preferred_element_type=F32)
                )
        explained = jnp.sum(total, axis=1, keepdims=True)
        post = prior_var - explained
        beta = 0.5 * (jnp.log(prior_var) - jnp.log(post))
        prec = beta / post
        share = prec - beta * (1.0 / prior_var)

        half = rows // 2
        for i, mean in enumerate(means):
            cols = slice(i * tri, (i + 1) * tri)
            value = mean * prec
            send[:half, cols] = value[:half].astype(BF16)
            keep[:half, cols] = value[half:]
        share_rows = [column_to_row(share[b * LANES : (b + 1) * LANES, :]) for b in range(blocks)]
        zeros = [jnp.zeros((1, out - half), F32)] if out > half else []
        row_send = jnp.concatenate(share_rows[:quarter] + zeros, axis=1)
        row_keep = jnp.concatenate(share_rows[quarter:] + zeros, axis=1)
        send[half:, :] = message_rows(row_send)
        keep[half:, :] = pick_rows((row_keep,), EXTRA, out)

    return kernel


def message_rows(row):
    high = row.astype(BF16).astype(F32)
    return pick_rows((high, row - high), EXTRA, row.shape[1]).astype(BF16)


def in_vmem(value):
    return pltpu.with_memory_space_constraint(value, pltpu.VMEM)


def expert_half(near_half, ids, cand, train, inv, wts):
    dims, runs, out = train.shape[1], wts.shape[1], wts.shape[2]
    rows = ids.shape[0] * LANES // 2
    vmem = pl.BlockSpec(memory_space=pltpu.VMEM)
    hbm = pl.BlockSpec(memory_space=pl.ANY)
    shape = (rows // 2 + EXTRA, out)
    return pl.pallas_call(
        make_experts_kernel(near_half),
        in_specs=[hbm] * 5,
        out_specs=[vmem, vmem],
        out_shape=[pltpu.VMEM(shape, BF16), pltpu.VMEM(shape, F32)],
        scratch_shapes=[
            pltpu.VMEM(ids.shape, jnp.int32),
            pltpu.VMEM(cand.shape, F32),
            pltpu.VMEM((dims, runs), F32),
            pltpu.VMEM((runs, runs), F32),
            pltpu.VMEM((runs, out), F32),
            pltpu.VMEM((LANES, runs), BF16),
            pltpu.VMEM((rows, runs), BF16),
            pltpu.VMEM((rows, runs), BF16),
            pltpu.SemaphoreType.DMA((4 + runs // 256,)),
        ],
        cost_estimate=pl.CostEstimate(
            flops=6 * rows * runs * (runs + out), transcendentals=rows * runs, bytes_accessed=8 * runs * runs
        ),
        name="experts_near" if near_half else "experts_far",
    )(ids, cand, train, inv, wts)


def add_parts(parts):
    keep = parts[0]
    rows = keep.shape[0] - EXTRA
    data = keep[:rows, :]
    row = keep[rows : rows + 1, :]
    for ref in parts[1:]:
        data = data + ref[:rows, :].astype(F32)
        low = ref[rows:, :].astype(F32)
        row = row + (low[0:1, :] + low[1:2, :])
    return data, row


def send_kernel(keep, recv, send):
    rows = keep.shape[0] - EXTRA
    data, row = add_parts((keep, recv))
    send[:rows, :] = data.astype(BF16)
    send[rows:, :] = message_rows(row)


def split_kernel(*refs):
    parts, (send, keep, data_s) = refs[:-3], refs[-3:]
    data, row = add_parts(parts)
    data_s[...] = data
    rows = send.shape[0] - EXTRA
    width = row.shape[1]
    _, _, mine = place()
    first = row[:, :rows]
    second = row[:, rows : 2 * rows]
    fill = [jnp.zeros((1, width - rows), F32)]
    row_keep = jnp.concatenate([jnp.where(mine == 0, first, second)] + fill, axis=1)
    row_send = jnp.concatenate([jnp.where(mine == 0, second, first)] + fill, axis=1)
    send[:rows, :] = data_s[pl.ds((1 - mine) * rows, rows), :].astype(BF16)
    send[rows:, :] = message_rows(row_send)
    keep[:rows, :] = data_s[pl.ds(mine * rows, rows), :]
    keep[rows:, :] = pick_rows((row_keep,), EXTRA, width)


def both_kernel(keep, recv, send, keep_out):
    rows = keep.shape[0] - EXTRA
    data, row = add_parts((keep, recv))
    send[:rows, :] = data.astype(BF16)
    send[rows:, :] = message_rows(row)
    keep_out[:rows, :] = data
    keep_out[rows:, :] = pick_rows((row,), EXTRA, row.shape[1])


def divide_kernel(keep, recv, coef):
    data, row = add_parts((keep, recv))
    total = row + 1.0 / prior_var
    for b in range(coef.shape[0] // LANES):
        at = slice(b * LANES, (b + 1) * LANES)
        column = row_to_column(total[:, at])[:, 0:1]
        coef[at, :] = (data[at] / column).astype(BF16)


def vmem_call(kernel, outs, *args, scratch=()):
    vmem = pl.BlockSpec(memory_space=pltpu.VMEM)
    return pl.pallas_call(
        kernel,
        in_specs=[vmem] * len(args),
        out_specs=[vmem] * len(outs),
        out_shape=[pltpu.VMEM(s, d) for s, d in outs],
        scratch_shapes=list(scratch),
    )(*[in_vmem(a) for a in args])


def make_field_kernel(places):
    def kernel(basis, clim, *refs):
        coefs = refs[: len(places)]
        out, buf, sem = refs[-3:]
        here = place()
        block = out.shape[0] // 8
        copies = []
        at = 0
        for i, (coef, (flips, offset)) in enumerate(zip(coefs, places)):
            rows = coef.shape[0]
            acc = jnp.dot(coef[...], basis[...], preferred_element_type=F32)
            buf[at : at + rows, :] = (acc + clim[...]).astype(BF16)
            bx, bc, by = [1 - h if f else h for h, f in zip(here, flips)]
            start = pl.multiple_of((bx * 4 + bc * 2 + by) * block + offset, rows)
            copy = pltpu.make_async_copy(buf.at[pl.ds(at, rows)], out.at[pl.ds(start, rows)], sem.at[i])
            copy.start()
            copies.append(copy)
            at += rows
        for copy in copies:
            copy.wait()

    return kernel


def field_rows(parts, basis, clim, tests, out=None):
    vmem = pl.BlockSpec(memory_space=pltpu.VMEM)
    hbm = pl.BlockSpec(memory_space=pl.ANY)
    cells = basis.shape[1]
    rows = sum(c.shape[0] for c, _, _ in parts)
    args = [in_vmem(v) for v in [basis, clim] + [c for c, _, _ in parts]]
    specs = [vmem] * len(args)
    alias = {}
    if out is not None:
        alias = {len(args): 0}
        args.append(out)
        specs.append(hbm)
    return pl.pallas_call(
        make_field_kernel([(flips, offset) for _, flips, offset in parts]),
        in_specs=specs,
        out_specs=hbm,
        out_shape=jax.ShapeDtypeStruct((tests, cells), BF16),
        input_output_aliases=alias,
        scratch_shapes=[pltpu.VMEM((rows, cells), BF16), pltpu.SemaphoreType.DMA((len(parts),))],
        cost_estimate=pl.CostEstimate(
            flops=2 * rows * basis.shape[0] * cells, transcendentals=0, bytes_accessed=2 * rows * cells
        ),
        name="field",
    )(*args)


def solution(mesh):
    n_group, n_expert = mesh.shape["group"], mesh.shape["expert"]
    assert n_group & (n_group - 1) == 0 and n_expert & (n_expert - 1) == 0
    assert n_group >= 2 and n_expert >= 4

    def swap(value, group_mask, expert_mask):
        pairs = []
        for g in range(n_group):
            for e in range(n_expert):
                pairs.append((g * n_expert + e, (g ^ group_mask) * n_expert + (e ^ expert_mask)))
        return lax.ppermute(value, AXES, pairs)

    core = (0, 1)
    far = (0, 2)
    near = (1, 0)
    adding = []
    for bit in range(2, n_expert.bit_length() - 1):
        adding.append((0, 1 << bit))
    for bit in range(1, n_group.bit_length() - 1):
        adding.append(((1 << (bit + 1)) - 2, 0))

    def work(train_inputs, inv_factor, weights, candidates, test_ids, basis, climatology):
        tests = test_ids.shape[0]
        out = weights.shape[2]
        block = tests // 8
        ids = test_ids.reshape(tests // LANES, 1, LANES)
        big = (2 * block + EXTRA, out)
        small = (block + EXTRA, out)

        send, keep = expert_half(False, ids, candidates, train_inputs, inv_factor, weights)
        got = swap(send, *core)
        (send,) = vmem_call(send_kernel, [(big, BF16)], keep, got)
        send, ids = lax.optimization_barrier((send, ids))
        got_x = swap(send, *far)
        send, keep = expert_half(True, ids, candidates, train_inputs, inv_factor, weights)
        got = swap(send, *core)
        send, keep = vmem_call(
            split_kernel, [(small, BF16), (small, F32)], keep, got, got_x, scratch=[pltpu.VMEM((2 * block, out), F32)]
        )
        got = swap(send, *near)
        for mask in adding:
            send, keep = vmem_call(both_kernel, [(small, BF16), (small, F32)], keep, got)
            got = swap(send, *mask)
        (coef,) = vmem_call(divide_kernel, [((block, out), BF16)], keep, got)

        clim = climatology.reshape(1, -1)
        half = block // 2
        by_x = swap(coef, *far)
        by_y = swap(coef, *near)
        by_c = swap(coef, *core)
        field = field_rows([(coef, (0, 0, 0), 0)], basis, clim, tests)
        diag_a = swap(by_x[:half], *near)
        diag_b = swap(by_y[half:], *far)
        by_cx = swap(by_x, *core)
        by_cy = swap(by_y, *core)
        field = field_rows(
            [(by_c, (0, 1, 0), 0), (by_x, (1, 0, 0), 0), (by_y, (0, 0, 1), 0)], basis, clim, tests, field
        )
        diag_ca = swap(diag_a, *core)
        diag_cb = swap(diag_b, *core)
        field = field_rows(
            [
                (by_cx, (1, 1, 0), 0),
                (by_cy, (0, 1, 1), 0),
                (diag_a, (1, 0, 1), 0),
                (diag_b, (1, 0, 1), half),
            ],
            basis,
            clim,
            tests,
            field,
        )
        return field_rows([(diag_ca, (1, 1, 1), 0), (diag_cb, (1, 1, 1), half)], basis, clim, tests, field)

    return jax.shard_map(
        work,
        mesh=mesh,
        in_specs=(
            P(AXES, None, None),
            P(AXES, None, None),
            P(AXES, None, None),
            P(),
            P(),
            P(None, AXES),
            P(AXES),
        ),
        out_specs=P(None, AXES),
        check_vma=False,
    )
```

profile of v0, /device:TPU:0, one launch (start us, length us, event | category | flops | bytes accessed | tf_op | source)
XLA Modules:
  0.0 58.6 jit_solution(12375870754287225488)
XLA Ops:
  0.0 6.5 %experts_far.1 = (bf16[264,512]{1,0:T(8,128)(2,1)S(1)}, f32[264,512]{1,0:T(8,128)S(1)}) custom-call(s32[8,1,128]{2,1,0:T(1,128)} %bitcast.6, f32[16,4096]{1,0:T(8,128)} %cand.3, f32[1,16,1024]{2,1,0:T(8,128)} %train.3, f32[1,1024,1024]{2,1,0:T(8,128)} %inv.3, f32[1,1024,512]{2,1,0:T(8,128)} %wts.3), custom_call_target="tpu_custom_call" | custom-call | flops 4831838208 | bytes 8388608 | tf_op jit(solution)/shard_map/experts_far/pallas_call | solution.py:178
  6.6 0.6 collective-permute-start
  7.1 1.2 %collective-permute-done.recv = bf16[264,512]{1,0:T(8,128)(2,1)S(1)} collective-permute-done((bf16[264,512]{1,0:T(8,128)(2,1)S(1)}, bf16[264,512]{1,0:T(8,128)(2,1)S(1)}, u32[]{:S(2)}, u32[]{:S(2)}) %collective-permute-start) | collective-permute-done | bytes 270368 | tf_op jit(solution)/shard_map/ppermute | solution.py:327
  8.3 0.1 shard_map.73
  8.4 6.6 %experts_near.1 = (bf16[264,512]{1,0:T(8,128)(2,1)S(1)}, f32[264,512]{1,0:T(8,128)S(1)}) custom-call(s32[8,1,128]{2,1,0:T(1,128)} %bitcast.7, f32[16,4096]{1,0:T(8,128)} %cand.3, f32[1,16,1024]{2,1,0:T(8,128)} %train.3, f32[1,1024,1024]{2,1,0:T(8,128)} %inv.3, f32[1,1024,512]{2,1,0:T(8,128)} %wts.3), custom_call_target="tpu_custom_call" | custom-call | flops 4831838208 | bytes 8388608 | tf_op jit(solution)/shard_map/experts_near/pallas_call | solution.py:178
  14.9 0.0 copy-start
  14.9 0.0 copy-start.1
  14.9 0.4 collective-permute-start.1
  15.4 2.6 %collective-permute-start.2 = (bf16[264,512]{1,0:T(8,128)(2,1)S(1)}, bf16[264,512]{1,0:T(8,128)(2,1)S(1)}, u32[]{:S(2)}, u32[]{:S(2)}) collective-permute-start(bf16[264,512]{1,0:T(8,128)(2,1)S(1)} %shard_map.73), channel_id=1, source_target_pairs={{0,2},{1,3},{2,0},{3,1},{4,6},{5,7},{6,4},{7,5},{8,10},{9,11},{10,... | collective-permute-start | bytes 811016 | tf_op jit(solution)/shard_map/ppermute | solution.py:327
  18.0 0.0 collective-permute-done.1.refs_1_
  18.0 7.0 %collective-permute-done.2.refs_2_ = bf16[264,512]{1,0:T(8,128)(2,1)S(1)} collective-permute-done((bf16[264,512]{1,0:T(8,128)(2,1)S(1)}, bf16[264,512]{1,0:T(8,128)(2,1)S(1)}, u32[]{:S(2)}, u32[]{:S(2)}) %collective-permute-start.2) | collective-permute-done | bytes 270368 | tf_op jit(solution)/shard_map/ppermute | solution.py:327
  25.0 0.2 shard_map.74
  25.2 1.8 %collective-permute-start.3 = (bf16[136,512]{1,0:T(8,128)(2,1)S(1)}, bf16[136,512]{1,0:T(8,128)(2,1)S(1)}, u32[]{:S(2)}, u32[]{:S(2)}) collective-permute-start(bf16[136,512]{1,0:T(8,128)(2,1)S(1)} %get-tuple-element.24), channel_id=1, source_target_pairs={{0,4},{1,5},{2,6},{3,7},{4,0},{5,1},{6,2},{7,3},{8,12},{9,13},{10,... | collective-permute-start | bytes 417800 | tf_op jit(solution)/shard_map/ppermute | solution.py:327
  27.0 3.6 %collective-permute-done.3.recv = bf16[136,512]{1,0:T(8,128)(2,1)S(1)} collective-permute-done((bf16[136,512]{1,0:T(8,128)(2,1)S(1)}, bf16[136,512]{1,0:T(8,128)(2,1)S(1)}, u32[]{:S(2)}, u32[]{:S(2)}) %collective-permute-start.3) | collective-permute-done | bytes 139296 | tf_op jit(solution)/shard_map/ppermute | solution.py:327
  30.7 1.6 %collective-permute-start.4 = (bf16[136,512]{1,0:T(8,128)(2,1)S(1)}, bf16[136,512]{1,0:T(8,128)(2,1)S(1)}, u32[]{:S(2)}, u32[]{:S(2)}) collective-permute-start(bf16[136,512]{1,0:T(8,128)(2,1)S(1)} %get-tuple-element.26), channel_id=1, source_target_pairs={{0,8},{1,9},{2,10},{3,11},{4,12},{5,13},{6,14},{7,15},{8,0},{9,1},... | collective-permute-start | bytes 417800 | tf_op jit(solution)/shard_map/ppermute | solution.py:327
  32.3 3.5 %collective-permute-done.4.recv = bf16[136,512]{1,0:T(8,128)(2,1)S(1)} collective-permute-done((bf16[136,512]{1,0:T(8,128)(2,1)S(1)}, bf16[136,512]{1,0:T(8,128)(2,1)S(1)}, u32[]{:S(2)}, u32[]{:S(2)}) %collective-permute-start.4) | collective-permute-done | bytes 139296 | tf_op jit(solution)/shard_map/ppermute | solution.py:327
  35.8 3.6 %collective-permute-start.5 = (bf16[136,512]{1,0:T(8,128)(2,1)S(1)}, bf16[136,512]{1,0:T(8,128)(2,1)S(1)}, u32[]{:S(2)}, u32[]{:S(2)}) collective-permute-start(bf16[136,512]{1,0:T(8,128)(2,1)S(1)} %get-tuple-element.28), channel_id=1, source_target_pairs={{0,24},{1,25},{2,26},{3,27},{4,28},{5,29},{6,30},{7,31},{8,16},{9,... | collective-permute-start | bytes 417800 | tf_op jit(solution)/shard_map/ppermute | solution.py:327
  39.5 3.4 %collective-permute-done.5.recv = bf16[136,512]{1,0:T(8,128)(2,1)S(1)} collective-permute-done((bf16[136,512]{1,0:T(8,128)(2,1)S(1)}, bf16[136,512]{1,0:T(8,128)(2,1)S(1)}, u32[]{:S(2)}, u32[]{:S(2)}) %collective-permute-start.5) | collective-permute-done | bytes 139296 | tf_op jit(solution)/shard_map/ppermute | solution.py:327
  42.9 0.2 shard_map.77.refs_0_
  43.0 1.5 %collective-permute-start.6 = (bf16[128,512]{1,0:T(8,128)(2,1)S(1)}, bf16[128,512]{1,0:T(8,128)(2,1)S(1)}, u32[]{:S(2)}, u32[]{:S(2)}) collective-permute-start(bf16[128,512]{1,0:T(8,128)(2,1)S(1)} %shard_map.77.refs_0_), channel_id=1, source_target_pairs={{0,2},{1,3},{2,0},{3,1},{4,6},{5,7},{6,4},{7,5},{8,10},{9,11},{10,... | collective-permute-start | bytes 393224 | tf_op jit(solution)/shard_map/ppermute | solution.py:327
  44.6 1.5 %collective-permute-start.9 = (bf16[128,512]{1,0:T(8,128)(2,1)S(1)}, bf16[128,512]{1,0:T(8,128)(2,1)S(1)}, u32[]{:S(2)}, u32[]{:S(2)}) collective-permute-start(bf16[128,512]{1,0:T(8,128)(2,1)S(1)} %shard_map.77.refs_0_), channel_id=1, source_target_pairs={{0,4},{1,5},{2,6},{3,7},{4,0},{5,1},{6,2},{7,3},{8,12},{9,13},{10,... | collective-permute-start | bytes 393224 | tf_op jit(solution)/shard_map/ppermute | solution.py:327
  46.1 0.0 collective-permute-start.14
  46.1 2.0 %collective-permute-done.6.refs_1_ = bf16[128,512]{1,0:T(8,128)(2,1)S(1)} collective-permute-done((bf16[128,512]{1,0:T(8,128)(2,1)S(1)}, bf16[128,512]{1,0:T(8,128)(2,1)S(1)}, u32[]{:S(2)}, u32[]{:S(2)}) %collective-permute-start.6) | collective-permute-done | bytes 131104 | tf_op jit(solution)/shard_map/ppermute | solution.py:327
  48.1 0.0 collective-permute-start.12
  48.1 1.5 %collective-permute-done.9.refs_2_ = bf16[128,512]{1,0:T(8,128)(2,1)S(1)} collective-permute-done((bf16[128,512]{1,0:T(8,128)(2,1)S(1)}, bf16[128,512]{1,0:T(8,128)(2,1)S(1)}, u32[]{:S(2)}, u32[]{:S(2)}) %collective-permute-start.9) | collective-permute-done | bytes 131104 | tf_op jit(solution)/shard_map/ppermute | solution.py:327
  49.5 0.0 collective-permute-start.13
  49.5 0.6 %collective-permute-start.10 = (bf16[64,512]{1,0:T(8,128)(2,1)S(1)}, bf16[64,512]{1,0:T(8,128)(2,1)S(1)}, u32[]{:S(2)}, u32[]{:S(2)}) collective-permute-start(bf16[64,512]{1,0:T(8,128)(2,1)S(1)} %slice.9), channel_id=1, source_target_pairs={{0,2},{1,3},{2,0},{3,1},{4,6},{5,7},{6,4},{7,5},{8,10},{9,11},{10,... | collective-permute-start | bytes 196616 | tf_op jit(solution)/shard_map/ppermute | solution.py:327
  50.2 1.5 %collective-permute-start.7 = (bf16[64,512]{1,0:T(8,128)(2,1)S(1)}, bf16[64,512]{1,0:T(8,128)(2,1)S(1)}, u32[]{:S(2)}, u32[]{:S(2)}) collective-permute-start(bf16[64,512]{1,0:T(8,128)(2,1)S(1)} %slice.8), channel_id=1, source_target_pairs={{0,4},{1,5},{2,6},{3,7},{4,0},{5,1},{6,2},{7,3},{8,12},{9,13},{10,... | collective-permute-start | bytes 196616 | tf_op jit(solution)/shard_map/ppermute | solution.py:327
  51.7 0.0 copy-done
  51.7 0.0 copy-done.1
  51.7 1.0 %field.4.refs_3_ = bf16[1024,1024]{1,0:T(8,128)(2,1)} custom-call(bf16[512,1024]{1,0:T(8,128)(2,1)S(1)} %copy-done, f32[1,1024]{1,0:T(1,128)S(1)} %bitcast.2, bf16[128,512]{1,0:T(8,128)(2,1)S(1)} %shard_map.77.refs_0_), custom_call_target="tpu_custom_call" | custom-call | flops 134217728 | bytes 262144 | tf_op jit(solution)/shard_map/field/pallas_call | solution.py:303
  52.7 1.3 %collective-permute-done.10.refs_3_ = bf16[64,512]{1,0:T(8,128)(2,1)S(1)} collective-permute-done((bf16[64,512]{1,0:T(8,128)(2,1)S(1)}, bf16[64,512]{1,0:T(8,128)(2,1)S(1)}, u32[]{:S(2)}, u32[]{:S(2)}) %collective-permute-start.10) | collective-permute-done | bytes 65568 | tf_op jit(solution)/shard_map/ppermute | solution.py:327
  54.1 0.0 collective-permute-start.11
  54.1 0.4 collective-permute-done.7.refs_2_
  54.5 0.1 collective-permute-start.8
  54.6 0.0 collective-permute-done.14.refs_0_
  54.6 1.3 %field.5.refs_4_ = bf16[1024,1024]{1,0:T(8,128)(2,1)} custom-call(bf16[512,1024]{1,0:T(8,128)(2,1)S(1)} %copy-done, f32[1,1024]{1,0:T(1,128)S(1)} %bitcast.3, bf16[128,512]{1,0:T(8,128)(2,1)S(1)} %collective-permute-done.14.refs_0_, bf16[128,512]{1,0:T(8,128)(2,1)S(1)} %collective-permute-done.6.refs_1_, ...), custom_call_target="tpu_custom_call", output_to_operand_aliasing={{}: (5, {})} | custom-call | flops 402653184 | bytes 786432 | tf_op jit(solution)/shard_map/field/pallas_call | solution.py:303
  55.9 0.0 collective-permute-done.12.refs_0_
  55.9 0.0 collective-permute-done.13.refs_1_
  55.9 1.5 %field.6.refs_2_ = bf16[1024,1024]{1,0:T(8,128)(2,1)} custom-call(bf16[512,1024]{1,0:T(8,128)(2,1)S(1)} %copy-done, f32[1,1024]{1,0:T(1,128)S(1)} %bitcast.4, bf16[128,512]{1,0:T(8,128)(2,1)S(1)} %collective-permute-done.12.refs_0_, bf16[128,512]{1,0:T(8,128)(2,1)S(1)} %collective-permute-done.13.refs_1_, ...), custom_call_target="tpu_custom_call", output_to_operand_aliasing={{}: (6, {})} | custom-call | flops 402653184 | bytes 786432 | tf_op jit(solution)/shard_map/field/pallas_call | solution.py:303
  57.4 0.0 collective-permute-done.11.refs_1_
  57.4 0.0 collective-permute-done.8.refs_0_
  57.4 1.2 %field.7 = bf16[1024,1024]{1,0:T(8,128)(2,1)} custom-call(bf16[512,1024]{1,0:T(8,128)(2,1)S(1)} %copy-done, f32[1,1024]{1,0:T(1,128)S(1)} %bitcast.5, bf16[64,512]{1,0:T(8,128)(2,1)S(1)} %collective-permute-done.8.refs_0_, bf16[64,512]{1,0:T(8,128)(2,1)S(1)} %collective-permute-done.11.refs_1_, ...), custom_call_target="tpu_custom_call", output_to_operand_aliasing={{}: (4, {})} | custom-call | flops 134217728 | bytes 262144 | tf_op jit(solution)/shard_map/field/pallas_call | solution.py:303
  (4 shorter events, 0.1 us)
Async XLA Ops:
  6.6 1.7 %collective-permute-start = (bf16[264,512]{1,0:T(8,128)(2,1)S(1)}, bf16[264,512]{1,0:T(8,128)(2,1)S(1)}, u32[]{:S(2)}, u32[]{:S(2)}) collective-permute-start(bf16[264,512]{1,0:T(8,128)(2,1)S(1)} %get-tuple-element.18), channel_id=1, source_target_pairs={{0,1},{1,0},{2,3},{3,2},{4,5},{5,4},{6,7},{7,6},{8,9},{9,8},{10,11... | collective-permute-start | bytes 811016 | tf_op jit(solution)/shard_map/ppermute | solution.py:327
  14.9 36.8 %copy-start = (bf16[512,1024]{1,0:T(8,128)(2,1)S(1)}, bf16[512,1024]{1,0:T(8,128)(2,1)}, u32[]{:S(2)}) copy-start(bf16[512,1024]{1,0:T(8,128)(2,1)} %basis.7) | copy-start | bytes 3145732
  14.9 36.8 %copy-start.1 = (f32[1024]{0:T(1024)S(1)}, f32[1024]{0:T(1024)}, u32[]{:S(2)}) copy-start(f32[1024]{0:T(1024)} %param.13) | copy-start | bytes 12292
  14.9 3.1 %collective-permute-start.1 = (bf16[264,512]{1,0:T(8,128)(2,1)S(1)}, bf16[264,512]{1,0:T(8,128)(2,1)S(1)}, u32[]{:S(2)}, u32[]{:S(2)}) collective-permute-start(bf16[264,512]{1,0:T(8,128)(2,1)S(1)} %get-tuple-element.21), channel_id=1, source_target_pairs={{0,1},{1,0},{2,3},{3,2},{4,5},{5,4},{6,7},{7,6},{8,9},{9,8},{10,11... | collective-permute-start | bytes 811016 | tf_op jit(solution)/shard_map/ppermute | solution.py:327
  15.4 9.6 %collective-permute-start.2 = (bf16[264,512]{1,0:T(8,128)(2,1)S(1)}, bf16[264,512]{1,0:T(8,128)(2,1)S(1)}, u32[]{:S(2)}, u32[]{:S(2)}) collective-permute-start(bf16[264,512]{1,0:T(8,128)(2,1)S(1)} %shard_map.73), channel_id=1, source_target_pairs={{0,2},{1,3},{2,0},{3,1},{4,6},{5,7},{6,4},{7,5},{8,10},{9,11},{10,... | collective-permute-start | bytes 811016 | tf_op jit(solution)/shard_map/ppermute | solution.py:327
  25.2 5.4 %collective-permute-start.3 = (bf16[136,512]{1,0:T(8,128)(2,1)S(1)}, bf16[136,512]{1,0:T(8,128)(2,1)S(1)}, u32[]{:S(2)}, u32[]{:S(2)}) collective-permute-start(bf16[136,512]{1,0:T(8,128)(2,1)S(1)} %get-tuple-element.24), channel_id=1, source_target_pairs={{0,4},{1,5},{2,6},{3,7},{4,0},{5,1},{6,2},{7,3},{8,12},{9,13},{10,... | collective-permute-start | bytes 417800 | tf_op jit(solution)/shard_map/ppermute | solution.py:327
  30.7 5.1 %collective-permute-start.4 = (bf16[136,512]{1,0:T(8,128)(2,1)S(1)}, bf16[136,512]{1,0:T(8,128)(2,1)S(1)}, u32[]{:S(2)}, u32[]{:S(2)}) collective-permute-start(bf16[136,512]{1,0:T(8,128)(2,1)S(1)} %get-tuple-element.26), channel_id=1, source_target_pairs={{0,8},{1,9},{2,10},{3,11},{4,12},{5,13},{6,14},{7,15},{8,0},{9,1},... | collective-permute-start | bytes 417800 | tf_op jit(solution)/shard_map/ppermute | solution.py:327
  35.8 7.0 %collective-permute-start.5 = (bf16[136,512]{1,0:T(8,128)(2,1)S(1)}, bf16[136,512]{1,0:T(8,128)(2,1)S(1)}, u32[]{:S(2)}, u32[]{:S(2)}) collective-permute-start(bf16[136,512]{1,0:T(8,128)(2,1)S(1)} %get-tuple-element.28), channel_id=1, source_target_pairs={{0,24},{1,25},{2,26},{3,27},{4,28},{5,29},{6,30},{7,31},{8,16},{9,... | collective-permute-start | bytes 417800 | tf_op jit(solution)/shard_map/ppermute | solution.py:327
  43.0 5.0 %collective-permute-start.6 = (bf16[128,512]{1,0:T(8,128)(2,1)S(1)}, bf16[128,512]{1,0:T(8,128)(2,1)S(1)}, u32[]{:S(2)}, u32[]{:S(2)}) collective-permute-start(bf16[128,512]{1,0:T(8,128)(2,1)S(1)} %shard_map.77.refs_0_), channel_id=1, source_target_pairs={{0,2},{1,3},{2,0},{3,1},{4,6},{5,7},{6,4},{7,5},{8,10},{9,11},{10,... | collective-permute-start | bytes 393224 | tf_op jit(solution)/shard_map/ppermute | solution.py:327
  44.6 5.0 %collective-permute-start.9 = (bf16[128,512]{1,0:T(8,128)(2,1)S(1)}, bf16[128,512]{1,0:T(8,128)(2,1)S(1)}, u32[]{:S(2)}, u32[]{:S(2)}) collective-permute-start(bf16[128,512]{1,0:T(8,128)(2,1)S(1)} %shard_map.77.refs_0_), channel_id=1, source_target_pairs={{0,4},{1,5},{2,6},{3,7},{4,0},{5,1},{6,2},{7,3},{8,12},{9,13},{10,... | collective-permute-start | bytes 393224 | tf_op jit(solution)/shard_map/ppermute | solution.py:327
  46.1 8.5 %collective-permute-start.14 = (bf16[128,512]{1,0:T(8,128)(2,1)S(1)}, bf16[128,512]{1,0:T(8,128)(2,1)S(1)}, u32[]{:S(2)}, u32[]{:S(2)}) collective-permute-start(bf16[128,512]{1,0:T(8,128)(2,1)S(1)} %shard_map.77.refs_0_), channel_id=1, source_target_pairs={{0,1},{1,0},{2,3},{3,2},{4,5},{5,4},{6,7},{7,6},{8,9},{9,8},{10,11... | collective-permute-start | bytes 393224 | tf_op jit(solution)/shard_map/ppermute | solution.py:327
  48.1 7.8 %collective-permute-start.12 = (bf16[128,512]{1,0:T(8,128)(2,1)S(1)}, bf16[128,512]{1,0:T(8,128)(2,1)S(1)}, u32[]{:S(2)}, u32[]{:S(2)}) collective-permute-start(bf16[128,512]{1,0:T(8,128)(2,1)S(1)} %collective-permute-done.6.refs_1_), channel_id=1, source_target_pairs={{0,1},{1,0},{2,3},{3,2},{4,5},{5,4},{6,7},{7,6},{8,9},{9,8},{10,11... | collective-permute-start | bytes 393224 | tf_op jit(solution)/shard_map/ppermute | solution.py:327
  49.5 6.4 %collective-permute-start.13 = (bf16[128,512]{1,0:T(8,128)(2,1)S(1)}, bf16[128,512]{1,0:T(8,128)(2,1)S(1)}, u32[]{:S(2)}, u32[]{:S(2)}) collective-permute-start(bf16[128,512]{1,0:T(8,128)(2,1)S(1)} %collective-permute-done.9.refs_2_), channel_id=1, source_target_pairs={{0,1},{1,0},{2,3},{3,2},{4,5},{5,4},{6,7},{7,6},{8,9},{9,8},{10,11... | collective-permute-start | bytes 393224 | tf_op jit(solution)/shard_map/ppermute | solution.py:327
  49.5 4.5 %collective-permute-start.10 = (bf16[64,512]{1,0:T(8,128)(2,1)S(1)}, bf16[64,512]{1,0:T(8,128)(2,1)S(1)}, u32[]{:S(2)}, u32[]{:S(2)}) collective-permute-start(bf16[64,512]{1,0:T(8,128)(2,1)S(1)} %slice.9), channel_id=1, source_target_pairs={{0,2},{1,3},{2,0},{3,1},{4,6},{5,7},{6,4},{7,5},{8,10},{9,11},{10,... | collective-permute-start | bytes 196616 | tf_op jit(solution)/shard_map/ppermute | solution.py:327
  50.2 4.3 %collective-permute-start.7 = (bf16[64,512]{1,0:T(8,128)(2,1)S(1)}, bf16[64,512]{1,0:T(8,128)(2,1)S(1)}, u32[]{:S(2)}, u32[]{:S(2)}) collective-permute-start(bf16[64,512]{1,0:T(8,128)(2,1)S(1)} %slice.8), channel_id=1, source_target_pairs={{0,4},{1,5},{2,6},{3,7},{4,0},{5,1},{6,2},{7,3},{8,12},{9,13},{10,... | collective-permute-start | bytes 196616 | tf_op jit(solution)/shard_map/ppermute | solution.py:327
  54.1 3.4 %collective-permute-start.11 = (bf16[64,512]{1,0:T(8,128)(2,1)S(1)}, bf16[64,512]{1,0:T(8,128)(2,1)S(1)}, u32[]{:S(2)}, u32[]{:S(2)}) collective-permute-start(bf16[64,512]{1,0:T(8,128)(2,1)S(1)} %collective-permute-done.10.refs_3_), channel_id=1, source_target_pairs={{0,1},{1,0},{2,3},{3,2},{4,5},{5,4},{6,7},{7,6},{8,9},{9,8},{10,11... | collective-permute-start | bytes 196616 | tf_op jit(solution)/shard_map/ppermute | solution.py:327
  54.5 3.0 %collective-permute-start.8 = (bf16[64,512]{1,0:T(8,128)(2,1)S(1)}, bf16[64,512]{1,0:T(8,128)(2,1)S(1)}, u32[]{:S(2)}, u32[]{:S(2)}) collective-permute-start(bf16[64,512]{1,0:T(8,128)(2,1)S(1)} %collective-permute-done.7.refs_2_), channel_id=1, source_target_pairs={{0,1},{1,0},{2,3},{3,2},{4,5},{5,4},{6,7},{7,6},{8,9},{9,8},{10,11... | collective-permute-start | bytes 196616 | tf_op jit(solution)/shard_map/ppermute | solution.py:327
where the time goes:
time: 58.7 us; the launch traced here: 58.6 us
  waiting for transfers between devices  23.8 us (41%)
  Pallas kernels  18.6 us (32%)
  starting transfers between devices  16 us (27%)
    ppermute x15, waiting for transfers between devices, swap(): return lax.ppermute(value, AXES, pairs)  23.8 us
    ppermute x15, starting transfers between devices, swap(): return lax.ppermute(value, AXES, pairs)  16 us
    pallas_call x2, Pallas kernels, expert_half(): pl.pallas_call(make_experts_kernel(near_half), in_specs=[hbm] * 5, out_sp...  13.1 us
    pallas_call x4, Pallas kernels, field_rows(): pl.pallas_call(make_field_kernel([(flips, offset) for _, flips, offset in...  5.02 us
  transfers between devices with their start and end apart: 15, of which 9 were waited for; matrix products, arithmetic and copies ran while one was open for 0% of the time, Pallas kernels for 7%

commit v1 on v0

--- a/solution.py
+++ b/solution.py
@@ -218,7 +218,7 @@
 
 
 def split_kernel(*refs):
-    parts, (send, keep, data_s) = refs[:-3], refs[-3:]
+    parts, (send, same, keep, data_s) = refs[:-4], refs[-4:]
     data, row = add_parts(parts)
     data_s[...] = data
     rows = send.shape[0] - EXTRA
@@ -231,21 +231,26 @@
     row_send = jnp.concatenate([jnp.where(mine == 0, second, first)] + fill, axis=1)
     send[:rows, :] = data_s[pl.ds((1 - mine) * rows, rows), :].astype(BF16)
     send[rows:, :] = message_rows(row_send)
-    keep[:rows, :] = data_s[pl.ds(mine * rows, rows), :]
+    kept = data_s[pl.ds(mine * rows, rows), :]
+    keep[:rows, :] = kept
     keep[rows:, :] = pick_rows((row_keep,), EXTRA, width)
-
-
-def both_kernel(keep, recv, send, keep_out):
-    rows = keep.shape[0] - EXTRA
-    data, row = add_parts((keep, recv))
+    same[:rows, :] = kept.astype(BF16)
+    same[rows:, :] = message_rows(row_keep)
+
+
+def both_kernel(*refs):
+    parts, (send, keep_out) = refs[:-2], refs[-2:]
+    rows = keep_out.shape[0] - EXTRA
+    data, row = add_parts(parts)
     send[:rows, :] = data.astype(BF16)
     send[rows:, :] = message_rows(row)
     keep_out[:rows, :] = data
     keep_out[rows:, :] = pick_rows((row,), EXTRA, row.shape[1])
 
 
-def divide_kernel(keep, recv, coef):
-    data, row = add_parts((keep, recv))
+def divide_kernel(*refs):
+    coef = refs[-1]
+    data, row = add_parts(refs[:-1])
     total = row + 1.0 / prior_var
     for b in range(coef.shape[0] // LANES):
         at = slice(b * LANES, (b + 1) * LANES)
@@ -326,6 +331,9 @@
                 pairs.append((g * n_expert + e, (g ^ group_mask) * n_expert + (e ^ expert_mask)))
         return lax.ppermute(value, AXES, pairs)
 
+    def both_masks(a, b):
+        return a[0] ^ b[0], a[1] ^ b[1]
+
     core = (0, 1)
     far = (0, 2)
     near = (1, 0)
@@ -350,43 +358,36 @@
         got_x = swap(send, *far)
         send, keep = expert_half(True, ids, candidates, train_inputs, inv_factor, weights)
         got = swap(send, *core)
-        send, keep = vmem_call(
-            split_kernel, [(small, BF16), (small, F32)], keep, got, got_x, scratch=[pltpu.VMEM((2 * block, out), F32)]
+        send, same, keep = vmem_call(
+            split_kernel,
+            [(small, BF16), (small, BF16), (small, F32)],
+            keep,
+            got,
+            got_x,
+            scratch=[pltpu.VMEM((2 * block, out), F32)],
         )
-        got = swap(send, *near)
-        for mask in adding:
-            send, keep = vmem_call(both_kernel, [(small, BF16), (small, F32)], keep, got)
-            got = swap(send, *mask)
-        (coef,) = vmem_call(divide_kernel, [((block, out), BF16)], keep, got)
+        got_d = swap(send, *both_masks(near, adding[0]))
+        got_y = swap(send, *near)
+        got_z = swap(same, *adding[0])
+        parts = [keep, got_y, got_z, got_d]
+        for mask in adding[1:]:
+            send, keep = vmem_call(both_kernel, [(small, BF16), (small, F32)], *parts)
+            parts = [keep, swap(send, *mask)]
+        (coef,) = vmem_call(divide_kernel, [((block, out), BF16)], *parts)
 
         clim = climatology.reshape(1, -1)
-        half = block // 2
+        by_d = swap(coef, *both_masks(far, near))
         by_x = swap(coef, *far)
         by_y = swap(coef, *near)
         by_c = swap(coef, *core)
-        field = field_rows([(coef, (0, 0, 0), 0)], basis, clim, tests)
-        diag_a = swap(by_x[:half], *near)
-        diag_b = swap(by_y[half:], *far)
+        field = field_rows([(coef, (0, 0, 0), 0), (by_c, (0, 1, 0), 0)], basis, clim, tests)
         by_cx = swap(by_x, *core)
         by_cy = swap(by_y, *core)
-        field = field_rows(
-            [(by_c, (0, 1, 0), 0), (by_x, (1, 0, 0), 0), (by_y, (0, 0, 1), 0)], basis, clim, tests, field
-        )
-        diag_ca = swap(diag_a, *core)
-        diag_cb = swap(diag_b, *core)
-        field = field_rows(
-            [
-                (by_cx, (1, 1, 0), 0),
-                (by_cy, (0, 1, 1), 0),
-                (diag_a, (1, 0, 1), 0),
-                (diag_b, (1, 0, 1), half),
-            ],
-            basis,
-            clim,
-            tests,
-            field,
-        )
-        return field_rows([(diag_ca, (1, 1, 1), 0), (diag_cb, (1, 1, 1), half)], basis, clim, tests, field)
+        field = field_rows([(by_x, (1, 0, 0), 0), (by_y, (0, 0, 1), 0)], basis, clim, tests, field)
+        by_cd = swap(by_d, *core)
+        parts = [(by_cx, (1, 1, 0), 0), (by_cy, (0, 1, 1), 0), (by_d, (1, 0, 1), 0)]
+        field = field_rows(parts, basis, clim, tests, field)
+        return field_rows([(by_cd, (1, 1, 1), 0)], basis, clim, tests, field)
 
     return jax.shard_map(
         work,

time: 58.7 us -> 56 us (0.954)
  starting transfers between devices: 16 us -> 14.4 us
  waiting for transfers between devices: 23.8 us -> 23 us
    ppermute x15 -> x14, starting transfers between devices: 16 us -> 14.4 us  [swap(): return lax.ppermute(value, AXES, pairs)]
    ppermute x15 -> x14, waiting for transfers between devices: 23.8 us -> 23 us  [swap(): return lax.ppermute(value, AXES, pairs)]
  transfers between devices with their start and end apart: 15 -> 14, of which waited for: 9 -> 9; matrix products, arithmetic and copies ran while one was open for 0% -> 0% of each run, Pallas kernels for 7% -> 7%
where the time goes in v1:
time: 56 us; the launch traced here: 55.9 us
  waiting for transfers between devices  23 us (41%)
  Pallas kernels  18.3 us (33%)
  starting transfers between devices  14.4 us (26%)
    ppermute x14, waiting for transfers between devices, swap(): return lax.ppermute(value, AXES, pairs)  23 us
    ppermute x14, starting transfers between devices, swap(): return lax.ppermute(value, AXES, pairs)  14.4 us
    pallas_call x2, Pallas kernels, expert_half(): pl.pallas_call(make_experts_kernel(near_half), in_specs=[hbm] * 5, out_sp...  13.1 us
    pallas_call x4, Pallas kernels, field_rows(): pl.pallas_call(make_field_kernel([(flips, offset) for _, flips, offset in...  4.74 us
  transfers between devices with their start and end apart: 14, of which 9 were waited for; matrix products, arithmetic and copies ran while one was open for 0% of the time, Pallas kernels for 7%

profile of v1, /device:TPU:0, one launch (start us, length us, event | category | flops | bytes accessed | tf_op | source)
XLA Modules:
  0.0 55.9 jit_solution(3983921540442274894)
XLA Ops:
  0.0 6.5 %experts_far.1 = (bf16[264,512]{1,0:T(8,128)(2,1)S(1)}, f32[264,512]{1,0:T(8,128)S(1)}) custom-call(s32[8,1,128]{2,1,0:T(1,128)} %bitcast.6, f32[16,4096]{1,0:T(8,128)} %cand.3, f32[1,16,1024]{2,1,0:T(8,128)} %train.3, f32[1,1024,1024]{2,1,0:T(8,128)} %inv.3, f32[1,1024,512]{2,1,0:T(8,128)} %wts.3), custom_call_target="tpu_custom_call" | custom-call | flops 4831838208 | bytes 8388608 | tf_op jit(solution)/shard_map/experts_far/pallas_call | solution.py:178
  6.6 0.6 collective-permute-start
  7.1 1.2 %collective-permute-done.recv = bf16[264,512]{1,0:T(8,128)(2,1)S(1)} collective-permute-done((bf16[264,512]{1,0:T(8,128)(2,1)S(1)}, bf16[264,512]{1,0:T(8,128)(2,1)S(1)}, u32[]{:S(2)}, u32[]{:S(2)}) %collective-permute-start) | collective-permute-done | bytes 270368 | tf_op jit(solution)/shard_map/ppermute | solution.py:332
  8.3 0.1 shard_map.73
  8.4 6.6 %experts_near.1 = (bf16[264,512]{1,0:T(8,128)(2,1)S(1)}, f32[264,512]{1,0:T(8,128)S(1)}) custom-call(s32[8,1,128]{2,1,0:T(1,128)} %bitcast.7, f32[16,4096]{1,0:T(8,128)} %cand.3, f32[1,16,1024]{2,1,0:T(8,128)} %train.3, f32[1,1024,1024]{2,1,0:T(8,128)} %inv.3, f32[1,1024,512]{2,1,0:T(8,128)} %wts.3), custom_call_target="tpu_custom_call" | custom-call | flops 4831838208 | bytes 8388608 | tf_op jit(solution)/shard_map/experts_near/pallas_call | solution.py:178
  14.9 0.0 copy-start
  14.9 0.0 copy-start.1
  14.9 0.4 collective-permute-start.1
  15.4 2.6 %collective-permute-start.2 = (bf16[264,512]{1,0:T(8,128)(2,1)S(1)}, bf16[264,512]{1,0:T(8,128)(2,1)S(1)}, u32[]{:S(2)}, u32[]{:S(2)}) collective-permute-start(bf16[264,512]{1,0:T(8,128)(2,1)S(1)} %shard_map.73), channel_id=1, source_target_pairs={{0,2},{1,3},{2,0},{3,1},{4,6},{5,7},{6,4},{7,5},{8,10},{9,11},{10,... | collective-permute-start | bytes 811016 | tf_op jit(solution)/shard_map/ppermute | solution.py:332
  18.0 0.0 collective-permute-done.1.refs_1_
  18.0 7.0 %collective-permute-done.2.refs_2_ = bf16[264,512]{1,0:T(8,128)(2,1)S(1)} collective-permute-done((bf16[264,512]{1,0:T(8,128)(2,1)S(1)}, bf16[264,512]{1,0:T(8,128)(2,1)S(1)}, u32[]{:S(2)}, u32[]{:S(2)}) %collective-permute-start.2) | collective-permute-done | bytes 270368 | tf_op jit(solution)/shard_map/ppermute | solution.py:332
  25.0 0.2 shard_map.74
  25.2 1.8 %collective-permute-start.3 = (bf16[136,512]{1,0:T(8,128)(2,1)S(1)}, bf16[136,512]{1,0:T(8,128)(2,1)S(1)}, u32[]{:S(2)}, u32[]{:S(2)}) collective-permute-start(bf16[136,512]{1,0:T(8,128)(2,1)S(1)} %get-tuple-element.23), channel_id=1, source_target_pairs={{0,4},{1,5},{2,6},{3,7},{4,0},{5,1},{6,2},{7,3},{8,12},{9,13},{10,... | collective-permute-start | bytes 417800 | tf_op jit(solution)/shard_map/ppermute | solution.py:332
  27.0 1.5 %collective-permute-start.5 = (bf16[136,512]{1,0:T(8,128)(2,1)S(1)}, bf16[136,512]{1,0:T(8,128)(2,1)S(1)}, u32[]{:S(2)}, u32[]{:S(2)}) collective-permute-start(bf16[136,512]{1,0:T(8,128)(2,1)S(1)} %get-tuple-element.23), channel_id=1, source_target_pairs={{0,12},{1,13},{2,14},{3,15},{4,8},{5,9},{6,10},{7,11},{8,4},{9,5},... | collective-permute-start | bytes 417800 | tf_op jit(solution)/shard_map/ppermute | solution.py:332
  28.5 0.2 collective-permute-start.4
  28.7 4.0 %collective-permute-done.3.refs_1_ = bf16[136,512]{1,0:T(8,128)(2,1)S(1)} collective-permute-done((bf16[136,512]{1,0:T(8,128)(2,1)S(1)}, bf16[136,512]{1,0:T(8,128)(2,1)S(1)}, u32[]{:S(2)}, u32[]{:S(2)}) %collective-permute-start.3) | collective-permute-done | bytes 139296 | tf_op jit(solution)/shard_map/ppermute | solution.py:332
  32.7 1.5 %collective-permute-done.5.refs_3_ = bf16[136,512]{1,0:T(8,128)(2,1)S(1)} collective-permute-done((bf16[136,512]{1,0:T(8,128)(2,1)S(1)}, bf16[136,512]{1,0:T(8,128)(2,1)S(1)}, u32[]{:S(2)}, u32[]{:S(2)}) %collective-permute-start.5) | collective-permute-done | bytes 139296 | tf_op jit(solution)/shard_map/ppermute | solution.py:332
  34.3 0.6 collective-permute-done.4.refs_2_
  34.8 0.1 shard_map.75
  34.9 3.6 %collective-permute-start.6 = (bf16[136,512]{1,0:T(8,128)(2,1)S(1)}, bf16[136,512]{1,0:T(8,128)(2,1)S(1)}, u32[]{:S(2)}, u32[]{:S(2)}) collective-permute-start(bf16[136,512]{1,0:T(8,128)(2,1)S(1)} %get-tuple-element.26), channel_id=1, source_target_pairs={{0,24},{1,25},{2,26},{3,27},{4,28},{5,29},{6,30},{7,31},{8,16},{9,... | collective-permute-start | bytes 417800 | tf_op jit(solution)/shard_map/ppermute | solution.py:332
  38.6 3.4 %collective-permute-done.6.refs_1_ = bf16[136,512]{1,0:T(8,128)(2,1)S(1)} collective-permute-done((bf16[136,512]{1,0:T(8,128)(2,1)S(1)}, bf16[136,512]{1,0:T(8,128)(2,1)S(1)}, u32[]{:S(2)}, u32[]{:S(2)}) %collective-permute-start.6) | collective-permute-done | bytes 139296 | tf_op jit(solution)/shard_map/ppermute | solution.py:332
  41.9 0.2 shard_map.76.refs_0_
  42.1 1.5 %collective-permute-start.9 = (bf16[128,512]{1,0:T(8,128)(2,1)S(1)}, bf16[128,512]{1,0:T(8,128)(2,1)S(1)}, u32[]{:S(2)}, u32[]{:S(2)}) collective-permute-start(bf16[128,512]{1,0:T(8,128)(2,1)S(1)} %shard_map.76.refs_0_), channel_id=1, source_target_pairs={{0,2},{1,3},{2,0},{3,1},{4,6},{5,7},{6,4},{7,5},{8,10},{9,11},{10,... | collective-permute-start | bytes 393224 | tf_op jit(solution)/shard_map/ppermute | solution.py:332
  43.6 1.5 %collective-permute-start.11 = (bf16[128,512]{1,0:T(8,128)(2,1)S(1)}, bf16[128,512]{1,0:T(8,128)(2,1)S(1)}, u32[]{:S(2)}, u32[]{:S(2)}) collective-permute-start(bf16[128,512]{1,0:T(8,128)(2,1)S(1)} %shard_map.76.refs_0_), channel_id=1, source_target_pairs={{0,4},{1,5},{2,6},{3,7},{4,0},{5,1},{6,2},{7,3},{8,12},{9,13},{10,... | collective-permute-start | bytes 393224 | tf_op jit(solution)/shard_map/ppermute | solution.py:332
  45.2 0.5 collective-permute-start.7
  45.7 0.0 collective-permute-start.13
  45.7 1.7 %collective-permute-done.9.refs_0_ = bf16[128,512]{1,0:T(8,128)(2,1)S(1)} collective-permute-done((bf16[128,512]{1,0:T(8,128)(2,1)S(1)}, bf16[128,512]{1,0:T(8,128)(2,1)S(1)}, u32[]{:S(2)}, u32[]{:S(2)}) %collective-permute-start.9) | collective-permute-done | bytes 131104 | tf_op jit(solution)/shard_map/ppermute | solution.py:332
  47.3 0.0 collective-permute-start.10
  47.4 1.3 %collective-permute-done.11.refs_1_ = bf16[128,512]{1,0:T(8,128)(2,1)S(1)} collective-permute-done((bf16[128,512]{1,0:T(8,128)(2,1)S(1)}, bf16[128,512]{1,0:T(8,128)(2,1)S(1)}, u32[]{:S(2)}, u32[]{:S(2)}) %collective-permute-start.11) | collective-permute-done | bytes 131104 | tf_op jit(solution)/shard_map/ppermute | solution.py:332
  48.6 0.0 collective-permute-start.12
  48.6 2.4 %collective-permute-done.7.refs_2_ = bf16[128,512]{1,0:T(8,128)(2,1)S(1)} collective-permute-done((bf16[128,512]{1,0:T(8,128)(2,1)S(1)}, bf16[128,512]{1,0:T(8,128)(2,1)S(1)}, u32[]{:S(2)}, u32[]{:S(2)}) %collective-permute-start.7) | collective-permute-done | bytes 131104 | tf_op jit(solution)/shard_map/ppermute | solution.py:332
  51.0 0.0 collective-permute-start.8
  51.0 0.0 collective-permute-done.13.refs_1_
  51.1 0.0 copy-done
  51.1 0.0 copy-done.1
  51.1 1.2 %field.4.refs_2_ = bf16[1024,1024]{1,0:T(8,128)(2,1)} custom-call(bf16[512,1024]{1,0:T(8,128)(2,1)S(1)} %copy-done, f32[1,1024]{1,0:T(1,128)S(1)} %bitcast.2, bf16[128,512]{1,0:T(8,128)(2,1)S(1)} %shard_map.76.refs_0_, bf16[128,512]{1,0:T(8,128)(2,1)S(1)} %collective-permute-done.13.refs_1_), custom_call_target="tpu_custom_call" | custom-call | flops 268435456 | bytes 524288 | tf_op jit(solution)/shard_map/field/pallas_call | solution.py:308
  52.3 1.2 %field.5.refs_3_ = bf16[1024,1024]{1,0:T(8,128)(2,1)} custom-call(bf16[512,1024]{1,0:T(8,128)(2,1)S(1)} %copy-done, f32[1,1024]{1,0:T(1,128)S(1)} %bitcast.3, bf16[128,512]{1,0:T(8,128)(2,1)S(1)} %collective-permute-done.9.refs_0_, bf16[128,512]{1,0:T(8,128)(2,1)S(1)} %collective-permute-done.11.refs_1_, ...), custom_call_target="tpu_custom_call", output_to_operand_aliasing={{}: (4, {})} | custom-call | flops 268435456 | bytes 524288 | tf_op jit(solution)/shard_map/field/pallas_call | solution.py:308
  53.5 0.0 collective-permute-done.10.refs_0_
  53.5 0.0 collective-permute-done.12.refs_1_
  53.5 1.3 %field.6.refs_1_ = bf16[1024,1024]{1,0:T(8,128)(2,1)} custom-call(bf16[512,1024]{1,0:T(8,128)(2,1)S(1)} %copy-done, f32[1,1024]{1,0:T(1,128)S(1)} %bitcast.4, bf16[128,512]{1,0:T(8,128)(2,1)S(1)} %collective-permute-done.10.refs_0_, bf16[128,512]{1,0:T(8,128)(2,1)S(1)} %collective-permute-done.12.refs_1_, ...), custom_call_target="tpu_custom_call", output_to_operand_aliasing={{}: (5, {})} | custom-call | flops 402653184 | bytes 786432 | tf_op jit(solution)/shard_map/field/pallas_call | solution.py:308
  54.8 0.0 collective-permute-done.8.refs_0_
  54.8 1.0 %field.7 = bf16[1024,1024]{1,0:T(8,128)(2,1)} custom-call(bf16[512,1024]{1,0:T(8,128)(2,1)S(1)} %copy-done, f32[1,1024]{1,0:T(1,128)S(1)} %bitcast.5, bf16[128,512]{1,0:T(8,128)(2,1)S(1)} %collective-permute-done.8.refs_0_, bf16[1024,1024]{1,0:T(8,128)(2,1)} %field.6.refs_1_), custom_call_target="tpu_custom_call", output_to_operand_aliasing={{}: (3, {})} | custom-call | flops 134217728 | bytes 262144 | tf_op jit(solution)/shard_map/field/pallas_call | solution.py:308
Async XLA Ops:
  6.6 1.7 %collective-permute-start = (bf16[264,512]{1,0:T(8,128)(2,1)S(1)}, bf16[264,512]{1,0:T(8,128)(2,1)S(1)}, u32[]{:S(2)}, u32[]{:S(2)}) collective-permute-start(bf16[264,512]{1,0:T(8,128)(2,1)S(1)} %get-tuple-element.17), channel_id=1, source_target_pairs={{0,1},{1,0},{2,3},{3,2},{4,5},{5,4},{6,7},{7,6},{8,9},{9,8},{10,11... | collective-permute-start | bytes 811016 | tf_op jit(solution)/shard_map/ppermute | solution.py:332
  14.9 36.1 %copy-start = (bf16[512,1024]{1,0:T(8,128)(2,1)S(1)}, bf16[512,1024]{1,0:T(8,128)(2,1)}, u32[]{:S(2)}) copy-start(bf16[512,1024]{1,0:T(8,128)(2,1)} %basis.7) | copy-start | bytes 3145732
  14.9 36.1 %copy-start.1 = (f32[1024]{0:T(1024)S(1)}, f32[1024]{0:T(1024)}, u32[]{:S(2)}) copy-start(f32[1024]{0:T(1024)} %param.13) | copy-start | bytes 12292
  14.9 3.1 %collective-permute-start.1 = (bf16[264,512]{1,0:T(8,128)(2,1)S(1)}, bf16[264,512]{1,0:T(8,128)(2,1)S(1)}, u32[]{:S(2)}, u32[]{:S(2)}) collective-permute-start(bf16[264,512]{1,0:T(8,128)(2,1)S(1)} %get-tuple-element.20), channel_id=1, source_target_pairs={{0,1},{1,0},{2,3},{3,2},{4,5},{5,4},{6,7},{7,6},{8,9},{9,8},{10,11... | collective-permute-start | bytes 811016 | tf_op jit(solution)/shard_map/ppermute | solution.py:332
  15.4 9.6 %collective-permute-start.2 = (bf16[264,512]{1,0:T(8,128)(2,1)S(1)}, bf16[264,512]{1,0:T(8,128)(2,1)S(1)}, u32[]{:S(2)}, u32[]{:S(2)}) collective-permute-start(bf16[264,512]{1,0:T(8,128)(2,1)S(1)} %shard_map.73), channel_id=1, source_target_pairs={{0,2},{1,3},{2,0},{3,1},{4,6},{5,7},{6,4},{7,5},{8,10},{9,11},{10,... | collective-permute-start | bytes 811016 | tf_op jit(solution)/shard_map/ppermute | solution.py:332
  25.2 7.5 %collective-permute-start.3 = (bf16[136,512]{1,0:T(8,128)(2,1)S(1)}, bf16[136,512]{1,0:T(8,128)(2,1)S(1)}, u32[]{:S(2)}, u32[]{:S(2)}) collective-permute-start(bf16[136,512]{1,0:T(8,128)(2,1)S(1)} %get-tuple-element.23), channel_id=1, source_target_pairs={{0,4},{1,5},{2,6},{3,7},{4,0},{5,1},{6,2},{7,3},{8,12},{9,13},{10,... | collective-permute-start | bytes 417800 | tf_op jit(solution)/shard_map/ppermute | solution.py:332
  27.0 7.3 %collective-permute-start.5 = (bf16[136,512]{1,0:T(8,128)(2,1)S(1)}, bf16[136,512]{1,0:T(8,128)(2,1)S(1)}, u32[]{:S(2)}, u32[]{:S(2)}) collective-permute-start(bf16[136,512]{1,0:T(8,128)(2,1)S(1)} %get-tuple-element.23), channel_id=1, source_target_pairs={{0,12},{1,13},{2,14},{3,15},{4,8},{5,9},{6,10},{7,11},{8,4},{9,5},... | collective-permute-start | bytes 417800 | tf_op jit(solution)/shard_map/ppermute | solution.py:332
  28.5 6.3 %collective-permute-start.4 = (bf16[136,512]{1,0:T(8,128)(2,1)S(1)}, bf16[136,512]{1,0:T(8,128)(2,1)S(1)}, u32[]{:S(2)}, u32[]{:S(2)}) collective-permute-start(bf16[136,512]{1,0:T(8,128)(2,1)S(1)} %get-tuple-element.24), channel_id=1, source_target_pairs={{0,8},{1,9},{2,10},{3,11},{4,12},{5,13},{6,14},{7,15},{8,0},{9,1},... | collective-permute-start | bytes 417800 | tf_op jit(solution)/shard_map/ppermute | solution.py:332
  34.9 7.0 %collective-permute-start.6 = (bf16[136,512]{1,0:T(8,128)(2,1)S(1)}, bf16[136,512]{1,0:T(8,128)(2,1)S(1)}, u32[]{:S(2)}, u32[]{:S(2)}) collective-permute-start(bf16[136,512]{1,0:T(8,128)(2,1)S(1)} %get-tuple-element.26), channel_id=1, source_target_pairs={{0,24},{1,25},{2,26},{3,27},{4,28},{5,29},{6,30},{7,31},{8,16},{9,... | collective-permute-start | bytes 417800 | tf_op jit(solution)/shard_map/ppermute | solution.py:332
  42.1 5.2 %collective-permute-start.9 = (bf16[128,512]{1,0:T(8,128)(2,1)S(1)}, bf16[128,512]{1,0:T(8,128)(2,1)S(1)}, u32[]{:S(2)}, u32[]{:S(2)}) collective-permute-start(bf16[128,512]{1,0:T(8,128)(2,1)S(1)} %shard_map.76.refs_0_), channel_id=1, source_target_pairs={{0,2},{1,3},{2,0},{3,1},{4,6},{5,7},{6,4},{7,5},{8,10},{9,11},{10,... | collective-permute-start | bytes 393224 | tf_op jit(solution)/shard_map/ppermute | solution.py:332
  43.6 5.0 %collective-permute-start.11 = (bf16[128,512]{1,0:T(8,128)(2,1)S(1)}, bf16[128,512]{1,0:T(8,128)(2,1)S(1)}, u32[]{:S(2)}, u32[]{:S(2)}) collective-permute-start(bf16[128,512]{1,0:T(8,128)(2,1)S(1)} %shard_map.76.refs_0_), channel_id=1, source_target_pairs={{0,4},{1,5},{2,6},{3,7},{4,0},{5,1},{6,2},{7,3},{8,12},{9,13},{10,... | collective-permute-start | bytes 393224 | tf_op jit(solution)/shard_map/ppermute | solution.py:332
  45.2 5.9 %collective-permute-start.7 = (bf16[128,512]{1,0:T(8,128)(2,1)S(1)}, bf16[128,512]{1,0:T(8,128)(2,1)S(1)}, u32[]{:S(2)}, u32[]{:S(2)}) collective-permute-start(bf16[128,512]{1,0:T(8,128)(2,1)S(1)} %shard_map.76.refs_0_), channel_id=1, source_target_pairs={{0,6},{1,7},{2,4},{3,5},{4,2},{5,3},{6,0},{7,1},{8,14},{9,15},{10,... | collective-permute-start | bytes 393224 | tf_op jit(solution)/shard_map/ppermute | solution.py:332
  45.7 5.4 %collective-permute-start.13 = (bf16[128,512]{1,0:T(8,128)(2,1)S(1)}, bf16[128,512]{1,0:T(8,128)(2,1)S(1)}, u32[]{:S(2)}, u32[]{:S(2)}) collective-permute-start(bf16[128,512]{1,0:T(8,128)(2,1)S(1)} %shard_map.76.refs_0_), channel_id=1, source_target_pairs={{0,1},{1,0},{2,3},{3,2},{4,5},{5,4},{6,7},{7,6},{8,9},{9,8},{10,11... | collective-permute-start | bytes 393224 | tf_op jit(solution)/shard_map/ppermute | solution.py:332
  47.3 6.1 %collective-permute-start.10 = (bf16[128,512]{1,0:T(8,128)(2,1)S(1)}, bf16[128,512]{1,0:T(8,128)(2,1)S(1)}, u32[]{:S(2)}, u32[]{:S(2)}) collective-permute-start(bf16[128,512]{1,0:T(8,128)(2,1)S(1)} %collective-permute-done.9.refs_0_), channel_id=1, source_target_pairs={{0,1},{1,0},{2,3},{3,2},{4,5},{5,4},{6,7},{7,6},{8,9},{9,8},{10,11... | collective-permute-start | bytes 393224 | tf_op jit(solution)/shard_map/ppermute | solution.py:332
  48.6 4.9 %collective-permute-start.12 = (bf16[128,512]{1,0:T(8,128)(2,1)S(1)}, bf16[128,512]{1,0:T(8,128)(2,1)S(1)}, u32[]{:S(2)}, u32[]{:S(2)}) collective-permute-start(bf16[128,512]{1,0:T(8,128)(2,1)S(1)} %collective-permute-done.11.refs_1_), channel_id=1, source_target_pairs={{0,1},{1,0},{2,3},{3,2},{4,5},{5,4},{6,7},{7,6},{8,9},{9,8},{10,11... | collective-permute-start | bytes 393224 | tf_op jit(solution)/shard_map/ppermute | solution.py:332
  51.0 3.8 %collective-permute-start.8 = (bf16[128,512]{1,0:T(8,128)(2,1)S(1)}, bf16[128,512]{1,0:T(8,128)(2,1)S(1)}, u32[]{:S(2)}, u32[]{:S(2)}) collective-permute-start(bf16[128,512]{1,0:T(8,128)(2,1)S(1)} %collective-permute-done.7.refs_2_), channel_id=1, source_target_pairs={{0,1},{1,0},{2,3},{3,2},{4,5},{5,4},{6,7},{7,6},{8,9},{9,8},{10,11... | collective-permute-start | bytes 393224 | tf_op jit(solution)/shard_map/ppermute | solution.py:332

commit v2 on v1

v2 whole, which is shorter than its diff:
```python
import jax
import jax.numpy as jnp
from jax import lax
from jax.experimental import pallas as pl
from jax.experimental.pallas import tpu as pltpu
from jax.sharding import PartitionSpec as P


signal_var = 1.0
noise_var = 0.1
prior_var = signal_var + noise_var

AXES = ("group", "expert")
LANES = 128
LEAVING = ((1, 1), (1, 0), (0, 1))
STAYING = ((0, 0),)
TRI = 256
VMEM_LIMIT = 32 * 1024 * 1024
EXTRA = 8
F32 = jnp.float32
BF16 = jnp.bfloat16


def split3(v):
    a = v.astype(BF16).astype(F32)
    b = (v - a).astype(BF16).astype(F32)
    c = ((v - a) - b).astype(BF16).astype(F32)
    return a, b, c


def row_iota(shape):
    return lax.broadcasted_iota(jnp.int32, shape, 0)


def pick_rows(rows, count, width):
    at = row_iota((count, width))
    out = jnp.zeros((count, width), F32)
    for i, row in enumerate(rows):
        out = jnp.where(at == i, row, out)
    return out


def column_to_row(col):
    return jnp.transpose(jnp.broadcast_to(col, (LANES, LANES)))[0:1, :]


def row_to_column(row):
    return jnp.transpose(jnp.broadcast_to(row, (LANES, LANES)))


def place():
    expert = lax.axis_index("expert")
    group = lax.axis_index("group")
    return (expert >> 1) & 1, expert & 1, group & 1


def gathered(ident, cand):
    dims = cand.shape[0]
    low = jnp.broadcast_to(ident & (LANES - 1), (dims, LANES))
    high = jnp.broadcast_to(ident // LANES, (dims, LANES))
    q = jnp.zeros((dims, LANES), F32)
    for g in range(cand.shape[1] // LANES):
        part = jnp.take_along_axis(cand[:, g * LANES : (g + 1) * LANES], low, axis=1, mode="promise_in_bounds")
        q = jnp.where(high == g, part, q)
    return q


def query_side(q):
    dims = q.shape[0]
    q1, q2, q3 = split3(q)
    t1, t2, t3 = split3(-0.5 * jnp.sum(q * q, axis=0, keepdims=True))
    unit = jnp.ones((1, LANES), F32)
    side = pick_rows((unit, unit, unit, t1, t2, t3), 8, LANES)
    rest = jnp.zeros((LANES - 6 * dims - 8, LANES), F32)
    return jnp.transpose(jnp.concatenate((q1, q1, q2, q2, q1, q3, side, rest), axis=0)).astype(BF16)


def train_side(x):
    dims, runs = x.shape
    x1, x2, x3 = split3(x)
    s1, s2, s3 = split3(-0.5 * jnp.sum(x * x, axis=0, keepdims=True))
    one = jnp.ones((1, runs), F32)
    tail = pick_rows((s1, s2, s3, one, one, one), 8, runs)
    pad = jnp.zeros((LANES - 6 * dims - 8, runs), F32)
    return jnp.concatenate((x1, x2, x1, x2, x3, x1, tail, pad), axis=0).astype(BF16)


def fill_kernels(flips, ids, cand, x_ref, k1_s, k2_s):
    at_x, at_core, at_y = place()
    for b in range(k1_s.shape[0] // LANES):
        flip_x, flip_y = flips[b % len(flips)]
        x = 1 - at_x if flip_x else at_x
        y = 1 - at_y if flip_y else at_y
        c = at_core if b >= len(flips) else 1 - at_core
        lhs = query_side(gathered(ids[x * 4 + c * 2 + y], cand))
        kern = signal_var * jnp.exp(jnp.dot(lhs, x_ref[...], preferred_element_type=F32))
        k1 = kern.astype(BF16)
        at = pl.ds(b * LANES, LANES)
        k1_s[at, :] = k1
        k2_s[at, :] = (kern - k1.astype(F32)).astype(BF16)


def experts_terms(inv_parts, wts_parts, k1_s, k2_s, out, send, keep):
    rows, runs = k1_s.shape
    total = jnp.zeros((rows, LANES), F32)
    means = []
    nt_dims = (((1,), (1,)), ((), ()))
    for j in reversed(range(runs // TRI)):
        depth = (j + 1) * TRI
        a1, a2 = inv_parts(j)
        white = (
            lax.dot_general(k1_s[:, :depth], a1, nt_dims, preferred_element_type=F32)
            + lax.dot_general(k2_s[:, :depth], a1, nt_dims, preferred_element_type=F32)
            + lax.dot_general(k1_s[:, :depth], a2, nt_dims, preferred_element_type=F32)
        )
        square = white * white
        for i in range(TRI // LANES):
            total = total + square[:, i * LANES : (i + 1) * LANES]
        if len(means) * TRI < out:
            w = wts_parts(slice(len(means) * TRI, (len(means) + 1) * TRI))
            mean = jnp.dot(k1_s[...], w[0], preferred_element_type=F32)
            if len(w) > 1:
                mean = mean + jnp.dot(k2_s[...], w[0], preferred_element_type=F32)
                mean = mean + jnp.dot(k1_s[...], w[1], preferred_element_type=F32)
            means.append(mean)
    explained = jnp.sum(total, axis=1, keepdims=True)
    post = prior_var - explained
    beta = 0.5 * (jnp.log(prior_var) - jnp.log(post))
    prec = beta / post
    share = prec - beta * (1.0 / prior_var)

    half = rows // 2
    for i, mean in enumerate(means):
        cols = slice(i * TRI, (i + 1) * TRI)
        value = mean * prec
        send[:half, cols] = value[:half].astype(BF16)
        keep[:half, cols] = value[half:]
    blocks = rows // LANES
    share_rows = [column_to_row(share[b * LANES : (b + 1) * LANES, :]) for b in range(blocks)]
    zeros = [jnp.zeros((1, out - half), F32)] if out > half else []
    row_send = jnp.concatenate(share_rows[: blocks // 2] + zeros, axis=1)
    row_keep = jnp.concatenate(share_rows[blocks // 2 :] + zeros, axis=1)
    send[half:, :] = message_rows(row_send)
    keep[half:, :] = pick_rows((row_keep,), EXTRA, out)


def far_kernel(ids, cand, train, inv, wts, send, keep, x_o, a1_o, a2_o, w1_o, w2_o, *scratch):
    ids_s, cand_s, train_s, inv_s, w_s, k1_s, k2_s, sem = scratch
    runs, out = wts.shape[1], wts.shape[2]
    small = [
        pltpu.make_async_copy(train.at[0], train_s, sem.at[0]),
        pltpu.make_async_copy(ids, ids_s, sem.at[1]),
        pltpu.make_async_copy(cand, cand_s, sem.at[2]),
    ]
    big = [pltpu.make_async_copy(wts.at[0], w_s, sem.at[3])]
    for j in reversed(range(runs // TRI)):
        region = (pl.ds(j * TRI, TRI), pl.ds(0, (j + 1) * TRI))
        big.append(pltpu.make_async_copy(inv.at[(0,) + region], inv_s.at[region], sem.at[4 + j]))
    for copy in small + big:
        copy.start()
    small[0].wait()
    x_o[...] = train_side(train_s[...])
    small[1].wait()
    small[2].wait()
    fill_kernels(LEAVING, ids_s, cand_s, x_o, k1_s, k2_s)
    for copy in big:
        copy.wait()

    def inv_parts(j):
        depth = (j + 1) * TRI
        region = (slice(j * TRI, depth), slice(0, depth))
        a = inv_s[region]
        a1 = a.astype(BF16)
        a2 = (a - a1.astype(F32)).astype(BF16)
        a1_o[region] = a1
        a2_o[region] = a2
        return a1, a2

    def wts_parts(cols):
        w = w_s[:, cols]
        w1 = w.astype(BF16)
        w1_o[:, cols] = w1
        w2_o[:, cols] = (w - w1.astype(F32)).astype(BF16)
        return (w1,)

    experts_terms(inv_parts, wts_parts, k1_s, k2_s, out, send, keep)


def near_kernel(ids, cand, x_r, a1_r, a2_r, w1_r, w2_r, send, keep, k1_s, k2_s):
    fill_kernels(STAYING, ids, cand, x_r, k1_s, k2_s)

    def inv_parts(j):
        region = (slice(j * TRI, (j + 1) * TRI), slice(0, (j + 1) * TRI))
        return a1_r[region], a2_r[region]

    experts_terms(inv_parts, lambda cols: (w1_r[:, cols], w2_r[:, cols]), k1_s, k2_s, w1_r.shape[1], send, keep)


def message_rows(row):
    high = row.astype(BF16).astype(F32)
    return pick_rows((high, row - high), EXTRA, row.shape[1]).astype(BF16)


def in_vmem(value):
    return pltpu.with_memory_space_constraint(value, pltpu.VMEM)


def far_half(ids, cand, train, inv, wts):
    dims, runs, out = train.shape[1], wts.shape[1], wts.shape[2]
    rows = 2 * len(LEAVING) * LANES
    vmem = pl.BlockSpec(memory_space=pltpu.VMEM)
    hbm = pl.BlockSpec(memory_space=pltpu.HBM)
    shape = (rows // 2 + EXTRA, out)
    return pl.pallas_call(
        far_kernel,
        in_specs=[hbm] * 5,
        out_specs=[vmem] * 7,
        out_shape=[
            pltpu.VMEM(shape, BF16),
            pltpu.VMEM(shape, F32),
            pltpu.VMEM((LANES, runs), BF16),
            pltpu.VMEM((runs, runs), BF16),
            pltpu.VMEM((runs, runs), BF16),
            pltpu.VMEM((runs, out), BF16),
            pltpu.VMEM((runs, out), BF16),
        ],
        scratch_shapes=[
            pltpu.VMEM(ids.shape, jnp.int32),
            pltpu.VMEM(cand.shape, F32),
            pltpu.VMEM((dims, runs), F32),
            pltpu.VMEM((runs, runs), F32),
            pltpu.VMEM((runs, out), F32),
            pltpu.VMEM((rows, runs), BF16),
            pltpu.VMEM((rows, runs), BF16),
            pltpu.SemaphoreType.DMA((4 + runs // TRI,)),
        ],
        compiler_params=pltpu.CompilerParams(vmem_limit_bytes=VMEM_LIMIT),
        name="experts_far",
    )(*[in_hbm(v) for v in (ids, cand, train, inv, wts)])


def near_half(ids, cand, x_parts, inv1, inv2, wts1, wts2):
    runs, out = wts1.shape
    rows = 2 * len(STAYING) * LANES
    vmem = pl.BlockSpec(memory_space=pltpu.VMEM)
    shape = (rows // 2 + EXTRA, out)
    return pl.pallas_call(
        near_kernel,
        in_specs=[vmem] * 7,
        out_specs=[vmem] * 2,
        out_shape=[pltpu.VMEM(shape, BF16), pltpu.VMEM(shape, F32)],
        scratch_shapes=[pltpu.VMEM((rows, runs), BF16), pltpu.VMEM((rows, runs), BF16)],
        compiler_params=pltpu.CompilerParams(vmem_limit_bytes=VMEM_LIMIT),
        name="experts_near",
    )(*[in_vmem(v) for v in (ids, cand, x_parts, inv1, inv2, wts1, wts2)])


def add_parts(parts):
    keep = parts[0]
    rows = keep.shape[0] - EXTRA
    data = keep[:rows, :]
    row = keep[rows : rows + 1, :]
    for ref in parts[1:]:
        data = data + ref[:rows, :].astype(F32)
        low = ref[rows:, :].astype(F32)
        row = row + (low[0:1, :] + low[1:2, :])
    return data, row


def leave_kernel(keep, recv, *sends):
    data, row = add_parts((keep, recv))
    width = row.shape[1]
    for i, send in enumerate(sends):
        rows = send.shape[0] - EXTRA
        at = slice(i * rows, (i + 1) * rows)
        send[:rows, :] = data[at].astype(BF16)
        send[rows:, :] = message_rows(jnp.concatenate((row[:, at], jnp.zeros((1, width - rows), F32)), axis=1))


def both_kernel(*refs):
    parts, (send, keep_out) = refs[:-2], refs[-2:]
    rows = keep_out.shape[0] - EXTRA
    data, row = add_parts(parts)
    send[:rows, :] = data.astype(BF16)
    send[rows:, :] = message_rows(row)
    keep_out[:rows, :] = data
    keep_out[rows:, :] = pick_rows((row,), EXTRA, row.shape[1])


def divide_kernel(*refs):
    coef = refs[-1]
    data, row = add_parts(refs[:-1])
    total = row + 1.0 / prior_var
    for b in range(coef.shape[0] // LANES):
        at = slice(b * LANES, (b + 1) * LANES)
        column = row_to_column(total[:, at])[:, 0:1]
        coef[at, :] = (data[at] / column).astype(BF16)


def in_vmem(value):
    return pltpu.with_memory_space_constraint(value, pltpu.VMEM)


def in_hbm(value):
    return pltpu.with_memory_space_constraint(value, pltpu.HBM)


def vmem_call(kernel, outs, *args, scratch=()):
    vmem = pl.BlockSpec(memory_space=pltpu.VMEM)
    return pl.pallas_call(
        kernel,
        in_specs=[vmem] * len(args),
        out_specs=[vmem] * len(outs),
        out_shape=[pltpu.VMEM(s, d) for s, d in outs],
        scratch_shapes=list(scratch),
        compiler_params=pltpu.CompilerParams(vmem_limit_bytes=VMEM_LIMIT),
    )(*[in_vmem(a) for a in args])


def make_field_kernel(places):
    def kernel(basis, clim, *refs):
        coefs = refs[: len(places)]
        out, buf, sem = refs[-3:]
        here = place()
        block = out.shape[0] // 8
        copies = []
        at = 0
        for i, (coef, (flips, offset)) in enumerate(zip(coefs, places)):
            rows = coef.shape[0]
            acc = jnp.dot(coef[...], basis[...], preferred_element_type=F32)
            buf[at : at + rows, :] = (acc + clim[...]).astype(BF16)
            bx, bc, by = [1 - h if f else h for h, f in zip(here, flips)]
            start = pl.multiple_of((bx * 4 + bc * 2 + by) * block + offset, rows)
            copy = pltpu.make_async_copy(buf.at[pl.ds(at, rows)], out.at[pl.ds(start, rows)], sem.at[i])
            copy.start()
            copies.append(copy)
            at += rows
        for copy in copies:
            copy.wait()

    return kernel


def field_rows(parts, basis, clim, tests, out=None):
    vmem = pl.BlockSpec(memory_space=pltpu.VMEM)
    hbm = pl.BlockSpec(memory_space=pl.ANY)
    cells = basis.shape[1]
    rows = sum(c.shape[0] for c, _, _ in parts)
    args = [in_vmem(v) for v in [basis, clim] + [c for c, _, _ in parts]]
    specs = [vmem] * len(args)
    alias = {}
    if out is not None:
        alias = {len(args): 0}
        args.append(out)
        specs.append(hbm)
    return pl.pallas_call(
        make_field_kernel([(flips, offset) for _, flips, offset in parts]),
        in_specs=specs,
        out_specs=hbm,
        out_shape=jax.ShapeDtypeStruct((tests, cells), BF16),
        input_output_aliases=alias,
        scratch_shapes=[pltpu.VMEM((rows, cells), BF16), pltpu.SemaphoreType.DMA((len(parts),))],
        compiler_params=pltpu.CompilerParams(vmem_limit_bytes=VMEM_LIMIT),
        cost_estimate=pl.CostEstimate(
            flops=2 * rows * basis.shape[0] * cells, transcendentals=0, bytes_accessed=2 * rows * cells
        ),
        name="field",
    )(*args)


def solution(mesh):
    n_group, n_expert = mesh.shape["group"], mesh.shape["expert"]
    assert n_group & (n_group - 1) == 0 and n_expert & (n_expert - 1) == 0
    assert n_group >= 2 and n_expert >= 4

    def swap(value, group_mask, expert_mask):
        pairs = []
        for g in range(n_group):
            for e in range(n_expert):
                pairs.append((g * n_expert + e, (g ^ group_mask) * n_expert + (e ^ expert_mask)))
        return lax.ppermute(value, AXES, pairs)

    def both_masks(a, b):
        return a[0] ^ b[0], a[1] ^ b[1]

    core = (0, 1)
    far = (0, 2)
    near = (1, 0)
    adding = []
    for bit in range(2, n_expert.bit_length() - 1):
        adding.append((0, 1 << bit))
    for bit in range(1, n_group.bit_length() - 1):
        adding.append(((1 << (bit + 1)) - 2, 0))

    def work(train_inputs, inv_factor, weights, candidates, test_ids, basis, climatology):
        tests = test_ids.shape[0]
        out = weights.shape[2]
        block = tests // 8
        assert block == LANES
        ids = test_ids.reshape(tests // LANES, 1, LANES)
        small = (block + EXTRA, out)

        send, keep, *parts = far_half(ids, candidates, train_inputs, inv_factor, weights)
        got = swap(send, *core)
        leaving = vmem_call(leave_kernel, [(small, BF16)] * len(LEAVING), keep, got)
        got_d = swap(leaving[0], *both_masks(far, near))
        got_x = swap(leaving[1], *far)
        got_y = swap(leaving[2], *near)
        send, keep = near_half(ids, candidates, *parts)
        got = swap(send, *core)
        parts = [keep, got, got_x, got_y, got_d]
        for mask in adding:
            send, keep = vmem_call(both_kernel, [(small, BF16), (small, F32)], *parts)
            parts = [keep, swap(send, *mask)]
        (coef,) = vmem_call(divide_kernel, [((block, out), BF16)], *parts)

        clim = climatology.reshape(1, -1)
        by_d = swap(coef, *both_masks(far, near))
        by_x = swap(coef, *far)
        by_y = swap(coef, *near)
        by_c = swap(coef, *core)
        field = field_rows([(coef, (0, 0, 0), 0), (by_c, (0, 1, 0), 0)], basis, clim, tests)
        by_cx = swap(by_x, *core)
        by_cy = swap(by_y, *core)
        field = field_rows([(by_x, (1, 0, 0), 0), (by_y, (0, 0, 1), 0)], basis, clim, tests, field)
        by_cd = swap(by_d, *core)
        parts = [(by_cx, (1, 1, 0), 0), (by_cy, (0, 1, 1), 0), (by_d, (1, 0, 1), 0)]
        field = field_rows(parts, basis, clim, tests, field)
        return field_rows([(by_cd, (1, 1, 1), 0)], basis, clim, tests, field)

    return jax.shard_map(
        work,
        mesh=mesh,
        in_specs=(
            P(AXES, None, None),
            P(AXES, None, None),
            P(AXES, None, None),
            P(),
            P(),
            P(None, AXES),
            P(AXES),
        ),
        out_specs=P(None, AXES),
        check_vma=False,
    )
```

time: 56 us -> 47 us (0.84)
  waiting for transfers between devices: 23 us -> 18 us
  Pallas kernels: 18.3 us -> 14.6 us
    ppermute x14, waiting for transfers between devices: 23 us -> 18 us  [swap(): return lax.ppermute(value, AXES, pairs)]
    pallas_call x2, Pallas kernels: 13.1 us -> 9.44 us  [the longest x1 6.87 us: far_half(): pl.pallas_call(far_kernel, in_specs=[hbm] * 5, out_specs=[vmem] * 7, out_...]
  transfers between devices with their start and end apart: 14 -> 14, of which waited for: 9 -> 7; matrix products, arithmetic and copies ran while one was open for 0% -> 0% of each run, Pallas kernels for 7% -> 14%
where the time goes in v2:
time: 47 us; the launch traced here: 46.9 us
  waiting for transfers between devices  18 us (38%)
  Pallas kernels  14.6 us (31%)
  starting transfers between devices  14.1 us (30%)
    ppermute x14, waiting for transfers between devices, swap(): return lax.ppermute(value, AXES, pairs)  18 us
    ppermute x14, starting transfers between devices, swap(): return lax.ppermute(value, AXES, pairs)  14.1 us
    pallas_call x1, Pallas kernels, far_half(): pl.pallas_call(far_kernel, in_specs=[hbm] * 5, out_specs=[vmem] * 7, out_...  6.87 us
    pallas_call x4, Pallas kernels, field_rows(): pl.pallas_call(make_field_kernel([(flips, offset) for _, flips, offset in...  4.74 us
    pallas_call x1, Pallas kernels, near_half(): pl.pallas_call(near_kernel, in_specs=[vmem] * 7, out_specs=[vmem] * 2, ou...  2.57 us
  transfers between devices with their start and end apart: 14, of which 7 were waited for; matrix products, arithmetic and copies ran while one was open for 0% of the time, Pallas kernels for 14%

profile of v2, /device:TPU:0, one launch (start us, length us, event | category | flops | bytes accessed | tf_op | source)
XLA Modules:
  0.0 46.9 jit_solution(5766036192170402859)
XLA Ops:
  0.0 0.0 copy-start.1
  0.0 0.0 copy-start.3
  0.0 6.9 %experts_far.1 = (bf16[392,512]{1,0:T(8,128)(2,1)S(1)}, f32[392,512]{1,0:T(8,128)S(1)}, bf16[128,1024]{1,0:T(8,128)(2,1)S(1)}, bf16[1024,1024]{1,0:T(8,128)(2,1)...) custom-call(s32[8,1,128]{2,1,0:T(1,128)} %bitcast.6, ...), custom_call_target="tpu_custom_call" | custom-call | tf_op jit(solution)/shard_map/experts_far/pallas_call | solution.py:214
  6.9 0.6 %collective-permute-start.1 = (bf16[392,512]{1,0:T(8,128)(2,1)S(1)}, bf16[392,512]{1,0:T(8,128)(2,1)S(1)}, u32[]{:S(2)}, u32[]{:S(2)}) collective-permute-start(bf16[392,512]{1,0:T(8,128)(2,1)S(1)} %get-tuple-element.29), channel_id=1, source_target_pairs={{0,1},{1,0},{2,3},{3,2},{4,5},{5,4},{6,7},{7,6},{8,9},{9,8},{10,11... | collective-permute-start | bytes 1204232 | tf_op jit(solution)/shard_map/ppermute | solution.py:381
  7.4 0.0 copy-done.1
  7.4 0.0 copy-done.3
  7.4 2.6 %experts_near.1 = (bf16[136,512]{1,0:T(8,128)(2,1)S(1)}, f32[136,512]{1,0:T(8,128)S(1)}) custom-call(s32[8,1,128]{2,1,0:T(1,128)S(1)} %bitcast.7, f32[16,4096]{1,0:T(8,128)S(1)} %copy-done.1, bf16[128,1024]{1,0:T(8,128)(2,1)S(1)} %get-tuple-element.21.x_r, bf16[1024,1024]{1,0:T(8,128)(2,1)S(1)} %get-tuple-element.22.a1_r, ...), custom_call_target="tpu_custom_call" | custom-call | tf_op jit(solution)/shard_map/experts_near/pallas_call | solution.py:247
  10.0 0.0 copy-start
  10.0 0.0 copy-start.2
  10.0 0.1 collective-permute-start
  10.1 0.0 collective-permute-done.1.recv
  10.1 0.1 shard_map.73
  10.2 3.0 %collective-permute-start.2 = (bf16[136,512]{1,0:T(8,128)(2,1)S(1)}, bf16[136,512]{1,0:T(8,128)(2,1)S(1)}, u32[]{:S(2)}, u32[]{:S(2)}) collective-permute-start(bf16[136,512]{1,0:T(8,128)(2,1)S(1)} %get-tuple-element.30), channel_id=1, source_target_pairs={{0,2},{1,3},{2,0},{3,1},{4,6},{5,7},{6,4},{7,5},{8,10},{9,11},{10,... | collective-permute-start | bytes 417800 | tf_op jit(solution)/shard_map/ppermute | solution.py:381
  13.2 1.5 %collective-permute-start.3 = (bf16[136,512]{1,0:T(8,128)(2,1)S(1)}, bf16[136,512]{1,0:T(8,128)(2,1)S(1)}, u32[]{:S(2)}, u32[]{:S(2)}) collective-permute-start(bf16[136,512]{1,0:T(8,128)(2,1)S(1)} %get-tuple-element.31), channel_id=1, source_target_pairs={{0,4},{1,5},{2,6},{3,7},{4,0},{5,1},{6,2},{7,3},{8,12},{9,13},{10,... | collective-permute-start | bytes 417800 | tf_op jit(solution)/shard_map/ppermute | solution.py:381
  14.8 0.0 collective-permute-start.4
  14.8 0.0 collective-permute-done.refs_1_
  14.8 2.7 %collective-permute-done.2.refs_2_ = bf16[136,512]{1,0:T(8,128)(2,1)S(1)} collective-permute-done((bf16[136,512]{1,0:T(8,128)(2,1)S(1)}, bf16[136,512]{1,0:T(8,128)(2,1)S(1)}, u32[]{:S(2)}, u32[]{:S(2)}) %collective-permute-start.2) | collective-permute-done | bytes 139296 | tf_op jit(solution)/shard_map/ppermute | solution.py:381
  17.4 4.1 %collective-permute-done.3.refs_3_ = bf16[136,512]{1,0:T(8,128)(2,1)S(1)} collective-permute-done((bf16[136,512]{1,0:T(8,128)(2,1)S(1)}, bf16[136,512]{1,0:T(8,128)(2,1)S(1)}, u32[]{:S(2)}, u32[]{:S(2)}) %collective-permute-start.3) | collective-permute-done | bytes 139296 | tf_op jit(solution)/shard_map/ppermute | solution.py:381
  21.5 0.0 collective-permute-done.4.refs_4_
  21.5 0.1 shard_map.74
  21.7 1.6 %collective-permute-start.5 = (bf16[136,512]{1,0:T(8,128)(2,1)S(1)}, bf16[136,512]{1,0:T(8,128)(2,1)S(1)}, u32[]{:S(2)}, u32[]{:S(2)}) collective-permute-start(bf16[136,512]{1,0:T(8,128)(2,1)S(1)} %get-tuple-element.34), channel_id=1, source_target_pairs={{0,8},{1,9},{2,10},{3,11},{4,12},{5,13},{6,14},{7,15},{8,0},{9,1},... | collective-permute-start | bytes 417800 | tf_op jit(solution)/shard_map/ppermute | solution.py:381
  23.3 3.5 %collective-permute-done.5.refs_1_ = bf16[136,512]{1,0:T(8,128)(2,1)S(1)} collective-permute-done((bf16[136,512]{1,0:T(8,128)(2,1)S(1)}, bf16[136,512]{1,0:T(8,128)(2,1)S(1)}, u32[]{:S(2)}, u32[]{:S(2)}) %collective-permute-start.5) | collective-permute-done | bytes 139296 | tf_op jit(solution)/shard_map/ppermute | solution.py:381
  26.8 3.7 %collective-permute-start.6 = (bf16[136,512]{1,0:T(8,128)(2,1)S(1)}, bf16[136,512]{1,0:T(8,128)(2,1)S(1)}, u32[]{:S(2)}, u32[]{:S(2)}) collective-permute-start(bf16[136,512]{1,0:T(8,128)(2,1)S(1)} %get-tuple-element.36), channel_id=1, source_target_pairs={{0,24},{1,25},{2,26},{3,27},{4,28},{5,29},{6,30},{7,31},{8,16},{9,... | collective-permute-start | bytes 417800 | tf_op jit(solution)/shard_map/ppermute | solution.py:381
  30.5 3.4 %collective-permute-done.6.refs_1_ = bf16[136,512]{1,0:T(8,128)(2,1)S(1)} collective-permute-done((bf16[136,512]{1,0:T(8,128)(2,1)S(1)}, bf16[136,512]{1,0:T(8,128)(2,1)S(1)}, u32[]{:S(2)}, u32[]{:S(2)}) %collective-permute-start.6) | collective-permute-done | bytes 139296 | tf_op jit(solution)/shard_map/ppermute | solution.py:381
  33.9 0.2 shard_map.76.refs_0_
  34.0 1.6 %collective-permute-start.11 = (bf16[128,512]{1,0:T(8,128)(2,1)S(1)}, bf16[128,512]{1,0:T(8,128)(2,1)S(1)}, u32[]{:S(2)}, u32[]{:S(2)}) collective-permute-start(bf16[128,512]{1,0:T(8,128)(2,1)S(1)} %shard_map.76.refs_0_), channel_id=1, source_target_pairs={{0,4},{1,5},{2,6},{3,7},{4,0},{5,1},{6,2},{7,3},{8,12},{9,13},{10,... | collective-permute-start | bytes 393224 | tf_op jit(solution)/shard_map/ppermute | solution.py:381
  35.6 0.5 %collective-permute-start.9 = (bf16[128,512]{1,0:T(8,128)(2,1)S(1)}, bf16[128,512]{1,0:T(8,128)(2,1)S(1)}, u32[]{:S(2)}, u32[]{:S(2)}) collective-permute-start(bf16[128,512]{1,0:T(8,128)(2,1)S(1)} %shard_map.76.refs_0_), channel_id=1, source_target_pairs={{0,2},{1,3},{2,0},{3,1},{4,6},{5,7},{6,4},{7,5},{8,10},{9,11},{10,... | collective-permute-start | bytes 393224 | tf_op jit(solution)/shard_map/ppermute | solution.py:381
  36.2 1.4 %collective-permute-start.7 = (bf16[128,512]{1,0:T(8,128)(2,1)S(1)}, bf16[128,512]{1,0:T(8,128)(2,1)S(1)}, u32[]{:S(2)}, u32[]{:S(2)}) collective-permute-start(bf16[128,512]{1,0:T(8,128)(2,1)S(1)} %shard_map.76.refs_0_), channel_id=1, source_target_pairs={{0,6},{1,7},{2,4},{3,5},{4,2},{5,3},{6,0},{7,1},{8,14},{9,15},{10,... | collective-permute-start | bytes 393224 | tf_op jit(solution)/shard_map/ppermute | solution.py:381
  37.6 0.0 collective-permute-start.13
  37.6 1.5 %collective-permute-done.11.refs_1_ = bf16[128,512]{1,0:T(8,128)(2,1)S(1)} collective-permute-done((bf16[128,512]{1,0:T(8,128)(2,1)S(1)}, bf16[128,512]{1,0:T(8,128)(2,1)S(1)}, u32[]{:S(2)}, u32[]{:S(2)}) %collective-permute-start.11) | collective-permute-done | bytes 131104 | tf_op jit(solution)/shard_map/ppermute | solution.py:381
  39.1 0.0 collective-permute-start.12
  39.1 1.5 %collective-permute-done.9.refs_0_ = bf16[128,512]{1,0:T(8,128)(2,1)S(1)} collective-permute-done((bf16[128,512]{1,0:T(8,128)(2,1)S(1)}, bf16[128,512]{1,0:T(8,128)(2,1)S(1)}, u32[]{:S(2)}, u32[]{:S(2)}) %collective-permute-start.9) | collective-permute-done | bytes 131104 | tf_op jit(solution)/shard_map/ppermute | solution.py:381
  40.6 0.0 collective-permute-start.10
  40.6 1.4 %collective-permute-done.7.refs_2_ = bf16[128,512]{1,0:T(8,128)(2,1)S(1)} collective-permute-done((bf16[128,512]{1,0:T(8,128)(2,1)S(1)}, bf16[128,512]{1,0:T(8,128)(2,1)S(1)}, u32[]{:S(2)}, u32[]{:S(2)}) %collective-permute-start.7) | collective-permute-done | bytes 131104 | tf_op jit(solution)/shard_map/ppermute | solution.py:381
  42.0 0.0 collective-permute-start.8
  42.0 0.0 collective-permute-done.13.refs_1_
  42.0 0.0 copy-done
  42.0 0.0 copy-done.2
  42.1 1.2 %field.4.refs_2_ = bf16[1024,1024]{1,0:T(8,128)(2,1)} custom-call(bf16[512,1024]{1,0:T(8,128)(2,1)S(1)} %copy-done, f32[1,1024]{1,0:T(1,128)S(1)} %bitcast.2, bf16[128,512]{1,0:T(8,128)(2,1)S(1)} %shard_map.76.refs_0_, bf16[128,512]{1,0:T(8,128)(2,1)S(1)} %collective-permute-done.13.refs_1_), custom_call_target="tpu_custom_call" | custom-call | flops 268435456 | bytes 524288 | tf_op jit(solution)/shard_map/field/pallas_call | solution.py:356
  43.3 1.2 %field.5.refs_3_ = bf16[1024,1024]{1,0:T(8,128)(2,1)} custom-call(bf16[512,1024]{1,0:T(8,128)(2,1)S(1)} %copy-done, f32[1,1024]{1,0:T(1,128)S(1)} %bitcast.3, bf16[128,512]{1,0:T(8,128)(2,1)S(1)} %collective-permute-done.9.refs_0_, bf16[128,512]{1,0:T(8,128)(2,1)S(1)} %collective-permute-done.11.refs_1_, ...), custom_call_target="tpu_custom_call", output_to_operand_aliasing={{}: (4, {})} | custom-call | flops 268435456 | bytes 524288 | tf_op jit(solution)/shard_map/field/pallas_call | solution.py:356
  44.4 0.0 collective-permute-done.12.refs_1_
  44.5 0.0 collective-permute-done.10.refs_0_
  44.5 1.3 %field.6.refs_1_ = bf16[1024,1024]{1,0:T(8,128)(2,1)} custom-call(bf16[512,1024]{1,0:T(8,128)(2,1)S(1)} %copy-done, f32[1,1024]{1,0:T(1,128)S(1)} %bitcast.4, bf16[128,512]{1,0:T(8,128)(2,1)S(1)} %collective-permute-done.10.refs_0_, bf16[128,512]{1,0:T(8,128)(2,1)S(1)} %collective-permute-done.12.refs_1_, ...), custom_call_target="tpu_custom_call", output_to_operand_aliasing={{}: (5, {})} | custom-call | flops 402653184 | bytes 786432 | tf_op jit(solution)/shard_map/field/pallas_call | solution.py:356
  45.8 0.0 collective-permute-done.8.refs_0_
  45.8 1.0 %field.7 = bf16[1024,1024]{1,0:T(8,128)(2,1)} custom-call(bf16[512,1024]{1,0:T(8,128)(2,1)S(1)} %copy-done, f32[1,1024]{1,0:T(1,128)S(1)} %bitcast.5, bf16[128,512]{1,0:T(8,128)(2,1)S(1)} %collective-permute-done.8.refs_0_, bf16[1024,1024]{1,0:T(8,128)(2,1)} %field.6.refs_1_), custom_call_target="tpu_custom_call", output_to_operand_aliasing={{}: (3, {})} | custom-call | flops 134217728 | bytes 262144 | tf_op jit(solution)/shard_map/field/pallas_call | solution.py:356
  (1 shorter events, 0.0 us)
Async XLA Ops:
  0.0 7.4 %copy-start.1 = (f32[16,4096]{1,0:T(8,128)S(1)}, f32[16,4096]{1,0:T(8,128)}, u32[]{:S(2)}) copy-start(f32[16,4096]{1,0:T(8,128)} %cand.3) | copy-start | bytes 786436
  0.0 7.4 %copy-start.3 = (s32[1024]{0:T(1024)S(1)}, s32[1024]{0:T(1024)}, u32[]{:S(2)}) copy-start(s32[1024]{0:T(1024)} %param.11) | copy-start | bytes 12292
  6.9 3.2 %collective-permute-start.1 = (bf16[392,512]{1,0:T(8,128)(2,1)S(1)}, bf16[392,512]{1,0:T(8,128)(2,1)S(1)}, u32[]{:S(2)}, u32[]{:S(2)}) collective-permute-start(bf16[392,512]{1,0:T(8,128)(2,1)S(1)} %get-tuple-element.29), channel_id=1, source_target_pairs={{0,1},{1,0},{2,3},{3,2},{4,5},{5,4},{6,7},{7,6},{8,9},{9,8},{10,11... | collective-permute-start | bytes 1204232 | tf_op jit(solution)/shard_map/ppermute | solution.py:381
  10.0 32.0 %copy-start = (bf16[512,1024]{1,0:T(8,128)(2,1)S(1)}, bf16[512,1024]{1,0:T(8,128)(2,1)}, u32[]{:S(2)}) copy-start(bf16[512,1024]{1,0:T(8,128)(2,1)} %basis.7) | copy-start | bytes 3145732
  10.0 32.0 %copy-start.2 = (f32[1024]{0:T(1024)S(1)}, f32[1024]{0:T(1024)}, u32[]{:S(2)}) copy-start(f32[1024]{0:T(1024)} %param.13) | copy-start | bytes 12292
  10.0 4.8 %collective-permute-start = (bf16[136,512]{1,0:T(8,128)(2,1)S(1)}, bf16[136,512]{1,0:T(8,128)(2,1)S(1)}, u32[]{:S(2)}, u32[]{:S(2)}) collective-permute-start(bf16[136,512]{1,0:T(8,128)(2,1)S(1)} %get-tuple-element.27), channel_id=1, source_target_pairs={{0,1},{1,0},{2,3},{3,2},{4,5},{5,4},{6,7},{7,6},{8,9},{9,8},{10,11... | collective-permute-start | bytes 417800 | tf_op jit(solution)/shard_map/ppermute | solution.py:381
  10.2 7.2 %collective-permute-start.2 = (bf16[136,512]{1,0:T(8,128)(2,1)S(1)}, bf16[136,512]{1,0:T(8,128)(2,1)S(1)}, u32[]{:S(2)}, u32[]{:S(2)}) collective-permute-start(bf16[136,512]{1,0:T(8,128)(2,1)S(1)} %get-tuple-element.30), channel_id=1, source_target_pairs={{0,2},{1,3},{2,0},{3,1},{4,6},{5,7},{6,4},{7,5},{8,10},{9,11},{10,... | collective-permute-start | bytes 417800 | tf_op jit(solution)/shard_map/ppermute | solution.py:381
  13.2 8.3 %collective-permute-start.3 = (bf16[136,512]{1,0:T(8,128)(2,1)S(1)}, bf16[136,512]{1,0:T(8,128)(2,1)S(1)}, u32[]{:S(2)}, u32[]{:S(2)}) collective-permute-start(bf16[136,512]{1,0:T(8,128)(2,1)S(1)} %get-tuple-element.31), channel_id=1, source_target_pairs={{0,4},{1,5},{2,6},{3,7},{4,0},{5,1},{6,2},{7,3},{8,12},{9,13},{10,... | collective-permute-start | bytes 417800 | tf_op jit(solution)/shard_map/ppermute | solution.py:381
  14.8 6.8 %collective-permute-start.4 = (bf16[136,512]{1,0:T(8,128)(2,1)S(1)}, bf16[136,512]{1,0:T(8,128)(2,1)S(1)}, u32[]{:S(2)}, u32[]{:S(2)}) collective-permute-start(bf16[136,512]{1,0:T(8,128)(2,1)S(1)} %get-tuple-element.32), channel_id=1, source_target_pairs={{0,6},{1,7},{2,4},{3,5},{4,2},{5,3},{6,0},{7,1},{8,14},{9,15},{10,... | collective-permute-start | bytes 417800 | tf_op jit(solution)/shard_map/ppermute | solution.py:381
  21.7 5.1 %collective-permute-start.5 = (bf16[136,512]{1,0:T(8,128)(2,1)S(1)}, bf16[136,512]{1,0:T(8,128)(2,1)S(1)}, u32[]{:S(2)}, u32[]{:S(2)}) collective-permute-start(bf16[136,512]{1,0:T(8,128)(2,1)S(1)} %get-tuple-element.34), channel_id=1, source_target_pairs={{0,8},{1,9},{2,10},{3,11},{4,12},{5,13},{6,14},{7,15},{8,0},{9,1},... | collective-permute-start | bytes 417800 | tf_op jit(solution)/shard_map/ppermute | solution.py:381
  26.8 7.0 %collective-permute-start.6 = (bf16[136,512]{1,0:T(8,128)(2,1)S(1)}, bf16[136,512]{1,0:T(8,128)(2,1)S(1)}, u32[]{:S(2)}, u32[]{:S(2)}) collective-permute-start(bf16[136,512]{1,0:T(8,128)(2,1)S(1)} %get-tuple-element.36), channel_id=1, source_target_pairs={{0,24},{1,25},{2,26},{3,27},{4,28},{5,29},{6,30},{7,31},{8,16},{9,... | collective-permute-start | bytes 417800 | tf_op jit(solution)/shard_map/ppermute | solution.py:381
  34.0 5.0 %collective-permute-start.11 = (bf16[128,512]{1,0:T(8,128)(2,1)S(1)}, bf16[128,512]{1,0:T(8,128)(2,1)S(1)}, u32[]{:S(2)}, u32[]{:S(2)}) collective-permute-start(bf16[128,512]{1,0:T(8,128)(2,1)S(1)} %shard_map.76.refs_0_), channel_id=1, source_target_pairs={{0,4},{1,5},{2,6},{3,7},{4,0},{5,1},{6,2},{7,3},{8,12},{9,13},{10,... | collective-permute-start | bytes 393224 | tf_op jit(solution)/shard_map/ppermute | solution.py:381
  35.6 5.0 %collective-permute-start.9 = (bf16[128,512]{1,0:T(8,128)(2,1)S(1)}, bf16[128,512]{1,0:T(8,128)(2,1)S(1)}, u32[]{:S(2)}, u32[]{:S(2)}) collective-permute-start(bf16[128,512]{1,0:T(8,128)(2,1)S(1)} %shard_map.76.refs_0_), channel_id=1, source_target_pairs={{0,2},{1,3},{2,0},{3,1},{4,6},{5,7},{6,4},{7,5},{8,10},{9,11},{10,... | collective-permute-start | bytes 393224 | tf_op jit(solution)/shard_map/ppermute | solution.py:381
  36.2 5.9 %collective-permute-start.7 = (bf16[128,512]{1,0:T(8,128)(2,1)S(1)}, bf16[128,512]{1,0:T(8,128)(2,1)S(1)}, u32[]{:S(2)}, u32[]{:S(2)}) collective-permute-start(bf16[128,512]{1,0:T(8,128)(2,1)S(1)} %shard_map.76.refs_0_), channel_id=1, source_target_pairs={{0,6},{1,7},{2,4},{3,5},{4,2},{5,3},{6,0},{7,1},{8,14},{9,15},{10,... | collective-permute-start | bytes 393224 | tf_op jit(solution)/shard_map/ppermute | solution.py:381
  37.6 4.4 %collective-permute-start.13 = (bf16[128,512]{1,0:T(8,128)(2,1)S(1)}, bf16[128,512]{1,0:T(8,128)(2,1)S(1)}, u32[]{:S(2)}, u32[]{:S(2)}) collective-permute-start(bf16[128,512]{1,0:T(8,128)(2,1)S(1)} %shard_map.76.refs_0_), channel_id=1, source_target_pairs={{0,1},{1,0},{2,3},{3,2},{4,5},{5,4},{6,7},{7,6},{8,9},{9,8},{10,11... | collective-permute-start | bytes 393224 | tf_op jit(solution)/shard_map/ppermute | solution.py:381
  39.1 5.4 %collective-permute-start.12 = (bf16[128,512]{1,0:T(8,128)(2,1)S(1)}, bf16[128,512]{1,0:T(8,128)(2,1)S(1)}, u32[]{:S(2)}, u32[]{:S(2)}) collective-permute-start(bf16[128,512]{1,0:T(8,128)(2,1)S(1)} %collective-permute-done.11.refs_1_), channel_id=1, source_target_pairs={{0,1},{1,0},{2,3},{3,2},{4,5},{5,4},{6,7},{7,6},{8,9},{9,8},{10,11... | collective-permute-start | bytes 393224 | tf_op jit(solution)/shard_map/ppermute | solution.py:381
  40.6 3.9 %collective-permute-start.10 = (bf16[128,512]{1,0:T(8,128)(2,1)S(1)}, bf16[128,512]{1,0:T(8,128)(2,1)S(1)}, u32[]{:S(2)}, u32[]{:S(2)}) collective-permute-start(bf16[128,512]{1,0:T(8,128)(2,1)S(1)} %collective-permute-done.9.refs_0_), channel_id=1, source_target_pairs={{0,1},{1,0},{2,3},{3,2},{4,5},{5,4},{6,7},{7,6},{8,9},{9,8},{10,11... | collective-permute-start | bytes 393224 | tf_op jit(solution)/shard_map/ppermute | solution.py:381
  42.0 3.8 %collective-permute-start.8 = (bf16[128,512]{1,0:T(8,128)(2,1)S(1)}, bf16[128,512]{1,0:T(8,128)(2,1)S(1)}, u32[]{:S(2)}, u32[]{:S(2)}) collective-permute-start(bf16[128,512]{1,0:T(8,128)(2,1)S(1)} %collective-permute-done.7.refs_2_), channel_id=1, source_target_pairs={{0,1},{1,0},{2,3},{3,2},{4,5},{5,4},{6,7},{7,6},{8,9},{9,8},{10,11... | collective-permute-start | bytes 393224 | tf_op jit(solution)/shard_map/ppermute | solution.py:381
